TPU v7x, 32 devices: a whole 2x2x4 slice. The times are simulated.
32 devices in a mesh: elec: 4 (over y, core), pix: 8 (over z, x).
Axes of the slice: x: 2, y: 2, z: 4, core: 2. Of those that a mesh axis runs over, the one named last changes fastest.
Arguments:
- wavefronts: bfloat16 [1536, 2, 320, 256], P('elec', None, 'pix'), may hold values from -40 to 40, as said below
- trial_modes: float32 [2, 32, 320, 256], P(None, None, 'pix'), may hold values from -6 to 6
Outputs:
- sample_modes: float32 [2, 32, 320, 256], P(None, 'elec', None, 'pix')
Inputs may be any that keep to these rules, and one draw needn't show every extreme that they name: `wavefronts`: field samples of each electron's wavefront.
All inputs are finite; a program needn't handle non-finite values.
Results may differ from a plain program's by a relative error of at most 0.0075.
Values may be sent and summed in bfloat16 or wider, within the bound.
A program may use at most 128 MiB of HBM per device.

v0:
```python
import math

import jax
import jax.numpy as jnp
from jax import lax
from jax.sharding import PartitionSpec as P

ITERS = 2
NS_STEPS = 8


HIGH = lax.Precision.HIGHEST


def project(wave_re, wave_im, modes_low):
    stacked = modes_low.reshape(-1, modes_low.shape[2])
    swapped = jnp.concatenate([-modes_low[1], modes_low[0]], axis=0)
    contract = (((1,), (1,)), ((), ()))
    real_side = lax.dot_general(wave_re, stacked, contract, preferred_element_type=jnp.float32)
    imag_side = lax.dot_general(wave_im, swapped, contract, preferred_element_type=jnp.float32)
    return real_side + imag_side


def covariance(waves, projected, mode_count):
    pixels = waves.shape[1] // 2
    width = projected.shape[1]
    upper = projected.astype(jnp.bfloat16)
    lower = (projected - upper.astype(jnp.float32)).astype(jnp.bfloat16)
    both = jnp.concatenate([upper, lower], axis=1)
    stacked = lax.dot_general(
        both, waves, (((0,), (0,)), ((), ())), preferred_element_type=jnp.float32
    )
    blocks = stacked[:width] + stacked[width:]
    real_part = blocks[:mode_count, :pixels] + blocks[mode_count:, pixels:]
    imag_part = blocks[mode_count:, :pixels] - blocks[:mode_count, pixels:]
    return jnp.stack([real_part, imag_part])


def gram_matrix(fields):
    flat = fields.reshape(-1, fields.shape[2])
    return jnp.dot(flat, flat.T, precision=HIGH)


def lowdin(gram_raw, mode_count):
    gram_re = gram_raw[:mode_count, :mode_count] + gram_raw[mode_count:, mode_count:]
    gram_im = gram_raw[:mode_count, mode_count:] - gram_raw[mode_count:, :mode_count]
    embedded = jnp.concatenate(
        [jnp.concatenate([gram_re, -gram_im], 1), jnp.concatenate([gram_im, gram_re], 1)], 0
    )
    trace_value = jnp.trace(embedded)
    scaled = embedded / trace_value
    identity = jnp.eye(2 * mode_count, dtype=embedded.dtype)
    inverse_root = identity
    for iteration in range(NS_STEPS):
        correction = 1.5 * identity - 0.5 * jnp.dot(inverse_root, scaled, precision=HIGH)
        scaled = jnp.dot(scaled, correction, precision=HIGH)
        inverse_root = jnp.dot(correction, inverse_root, precision=HIGH)
    return (inverse_root / jnp.sqrt(trace_value)).T


def rotate(rotation, fields):
    flat = fields.reshape(-1, fields.shape[2])
    return jnp.dot(rotation, flat, precision=HIGH).reshape(fields.shape)


def dft_table(length):
    index = jnp.arange(length, dtype=jnp.int32)
    product = index[:, None] * index[None, :] % length
    angle = 2.0 * math.pi / length * product.astype(jnp.float32)
    return (jnp.cos(angle), -jnp.sin(angle))


def chirp_phase(row_pos, col_pos, row_total, col_total, factor):
    row_term = (row_pos - row_total / 2.0) ** 2 / row_total
    col_term = (col_pos - col_total / 2.0) ** 2 / col_total
    angle = math.pi * factor * (row_term[:, None] + col_term[None, :])
    return (jnp.cos(angle), jnp.sin(angle))


def column_section(field, row_pos, row_total, col_total):
    col_pos = jnp.arange(col_total, dtype=jnp.float32)
    chirp_re, chirp_im = chirp_phase(row_pos, col_pos, row_total, col_total, 0.5)
    launch_re = chirp_re * field[0] - chirp_im * field[1]
    launch_im = chirp_re * field[1] + chirp_im * field[0]
    table_re, table_im = dft_table(col_total)
    spec_re = jnp.einsum("mry,yv->mrv", launch_re, table_re, precision=HIGH) - jnp.einsum(
        "mry,yv->mrv", launch_im, table_im, precision=HIGH
    )
    spec_im = jnp.einsum("mry,yv->mrv", launch_re, table_im, precision=HIGH) + jnp.einsum(
        "mry,yv->mrv", launch_im, table_re, precision=HIGH
    )
    return jnp.stack([spec_re, spec_im])


def row_section(spectrum, col_pos, row_total, col_total):
    table_re, table_im = dft_table(row_total)
    out_re = jnp.einsum("ux,mxv->muv", table_re, spectrum[0], precision=HIGH) - jnp.einsum(
        "ux,mxv->muv", table_im, spectrum[1], precision=HIGH
    )
    out_im = jnp.einsum("ux,mxv->muv", table_re, spectrum[1], precision=HIGH) + jnp.einsum(
        "ux,mxv->muv", table_im, spectrum[0], precision=HIGH
    )
    row_pos = jnp.arange(row_total, dtype=jnp.float32)
    chirp_re, chirp_im = chirp_phase(row_pos, col_pos, row_total, col_total, 0.25)
    return jnp.stack([chirp_re * out_re - chirp_im * out_im, chirp_re * out_im + chirp_im * out_re])


def pixel_sum(partial_value):
    return lax.psum(partial_value, "pix")


def shards(wavefronts, trial_modes):
    electrons_dev, _, rows_dev, cols = wavefronts.shape
    mode_count = trial_modes.shape[1]
    pixels = rows_dev * cols
    groups = lax.axis_size("elec")
    mode_share = mode_count // groups
    waves = wavefronts.reshape(electrons_dev, 2 * pixels)
    wave_re = waves[:, :pixels]
    wave_im = waves[:, pixels:]
    modes = trial_modes.reshape(2, mode_count, pixels)
    projected_part = project(wave_re, wave_im, modes.astype(jnp.bfloat16))
    share_low = None
    share_modes = None
    for iteration in range(ITERS):
        if iteration > 0:
            projected_part = project(
                wave_re, wave_im, lax.all_gather(share_low, "elec", axis=2, tiled=True)
            )
        projected = pixel_sum(projected_part)
        applied_share = lax.psum_scatter(
            covariance(waves, projected, mode_count), "elec", scatter_dimension=2, tiled=True
        )
        gram_total = lax.psum(gram_matrix(applied_share), ("elec", "pix"))
        share_modes = rotate(lowdin(gram_total, mode_count), applied_share)
        share_low = share_modes.astype(jnp.bfloat16)
    local_modes = lax.all_to_all(share_modes, "elec", split_axis=1, concat_axis=2, tiled=True)
    field = local_modes.reshape(2, mode_share, rows_dev, cols)
    pix_count = lax.axis_size("pix")
    row_total = rows_dev * pix_count
    row_pos = (lax.axis_index("pix") * rows_dev + jnp.arange(rows_dev, dtype=jnp.int32)).astype(
        jnp.float32
    )
    spectrum = column_section(field, row_pos, row_total, cols)
    column_block = lax.all_to_all(spectrum, "pix", split_axis=3, concat_axis=2, tiled=True)
    col_width = column_block.shape[3]
    col_pos = (lax.axis_index("pix") * col_width + jnp.arange(col_width, dtype=jnp.int32)).astype(
        jnp.float32
    )
    return row_section(column_block, col_pos, row_total, cols)


def solution(mesh):
    in_specs = (P("elec", None, "pix", None), P(None, None, "pix", None))
    out_specs = P(None, "elec", None, "pix")
    return jax.shard_map(shards, mesh=mesh, in_specs=in_specs, out_specs=out_specs, check_vma=False)
```

profile of v0, /device:TPU:0, one launch (start us, length us, event | category | flops | bytes accessed | tf_op | source)
XLA Modules:
  0.0 470.5 jit_solution(15132005642279305516)
XLA Ops:
  6.5 11.1 %copy.19 = bf16[48,8,80,256]{3,1,2,0:T(8,128)(2,1)S(1)} copy(bf16[48,8,80,256]{3,2,1,0:T(8,128)(2,1)} %bitcast.196) | data formatting | bytes 31457280
  18.4 2.5 fusion.6
  23.2 3.2 fusion.27
  26.4 73.0 %all-reduce.3.cloned.1.call-done = f32[384,64]{0,1:T(8,128)} async-done(((f32[384,64]{0,1:T(8,128)}), f32[384,64]{0,1:T(8,128)}) %all-reduce.3.cloned.1.call-update) | async-done | bytes 98320 | tf_op jit(solution)/shard_map/psum | solution.py:109
  100.4 7.0 %fusion.98 = f32[128,20480]{1,0:T(8,128)S(1)} fusion(bf16[384,20480]{1,0:T(8,128)(2,1)} %bitcast.192, bf16[384,64]{0,1:T(8,128)(2,1)S(1)} %get-tuple-element.11, bf16[384,64]{0,1:T(8,128)(2,1)S(1)} %get-tuple-element.12), kind=kOutput, calls=%fused_computation.123 | convolution fusion | flops 2013462528 | bytes 26312704 | tf_op jit(solution)/shard_map/dot_general | solution.py:30
  110.0 33.6 %reduce-scatter.3.cloned.1.call-done = f32[2,32,2560]{2,1,0:T(8,128)} async-done(((f32[2,32,10240]{2,1,0:T(8,128)}), f32[2,32,2560]{2,1,0:T(8,128)}) %reduce-scatter.3.cloned.1.call-update) | async-done | bytes 655376 | tf_op jit(solution)/shard_map/reduce_scatter | solution.py:131
  145.7 39.4 %psum.29 = f32[64,64]{1,0:T(8,128)S(1)} all-reduce(f32[64,64]{1,0:T(8,128)S(1)} %fusion.152), channel_id=1, replica_groups=mesh['elec'=4,'pix'=8] {'elec','pix'}, use_global_device_ids=true, to_apply=%region_2.0 | all-reduce | flops 4096 | bytes 32768 | tf_op jit(solution)/shard_map/psum | solution.py:134
  193.7 18.8 %all-gather.2.cloned.1.call-done = bf16[2,32,10240]{2,1,0:T(8,128)(2,1)} async-done(((bf16[2,32,2560]{2,1,0:T(8,128)(2,1)}), bf16[2,32,10240]{2,1,0:T(8,128)(2,1)}) %all-gather.2.cloned.1.call-update) | async-done | bytes 1310736 | tf_op jit(solution)/shard_map/all_gather | solution.py:128
  213.8 5.9 %fusion = f32[64,384]{1,0:T(8,128)S(1)} fusion(bf16[384,20480]{1,0:T(8,128)(2,1)} %bitcast.193, bf16[32,10240]{1,0:T(8,128)(2,1)S(1)} %get-tuple-element.20, bf16[32,10240]{1,0:T(8,128)(2,1)S(1)} %get-tuple-element.19), kind=kOutput, calls=%fused_computation | convolution fusion | flops 505937920 | bytes 9273344 | tf_op jit(solution)/shard_map/dot_general | solution.py:20
  219.7 6.4 %fusion.35 = f32[384,64]{0,1:T(8,128)} fusion(f32[64,384]{1,0:T(8,128)S(1)} %fusion, bf16[64,10240]{1,0:T(8,128)(2,1)S(1)} %bitcast.208, bf16[384,20480]{1,0:T(8,128)(2,1)} %bitcast.194), kind=kOutput, calls=%fused_computation.38 | convolution fusion | flops 503341056 | bytes 9371648 | tf_op jit(solution)/shard_map/dot_general | solution.py:19
  226.2 70.3 %all-reduce.5.cloned.1.call-done = f32[384,64]{0,1:T(8,128)} async-done(((f32[384,64]{0,1:T(8,128)}), f32[384,64]{0,1:T(8,128)}) %all-reduce.5.cloned.1.call-update) | async-done | bytes 98320 | tf_op jit(solution)/shard_map/psum | solution.py:109
  297.5 7.0 %fusion.102 = f32[128,20480]{1,0:T(8,128)S(1)} fusion(bf16[384,20480]{1,0:T(8,128)(2,1)} %bitcast.195, bf16[384,64]{0,1:T(8,128)(2,1)S(1)} %get-tuple-element.7, bf16[384,64]{0,1:T(8,128)(2,1)S(1)} %get-tuple-element.8), kind=kOutput, calls=%fused_computation.127 | convolution fusion | flops 2013462528 | bytes 26312704 | tf_op jit(solution)/shard_map/dot_general | solution.py:30
  307.0 33.7 %reduce-scatter.5.cloned.1.call-done = f32[2,32,2560]{2,1,0:T(8,128)} async-done(((f32[2,32,10240]{2,1,0:T(8,128)}), f32[2,32,2560]{2,1,0:T(8,128)}) %reduce-scatter.5.cloned.1.call-update) | async-done | bytes 655376 | tf_op jit(solution)/shard_map/reduce_scatter | solution.py:131
  342.8 39.4 %psum.31 = f32[64,64]{1,0:T(8,128)S(1)} all-reduce(f32[64,64]{1,0:T(8,128)S(1)} %fusion.165), channel_id=1, replica_groups=mesh['elec'=4,'pix'=8] {'elec','pix'}, use_global_device_ids=true, to_apply=%region_6.7 | all-reduce | flops 4096 | bytes 32768 | tf_op jit(solution)/shard_map/psum | solution.py:134
  391.1 4.0 all-to-all-start
  395.4 9.9 %all-to-all-done = f32[2,32,2560]{2,0,1:T(2,128)S(1)} async-done(((f32[2,32,2560]{2,0,1:T(2,128)}), f32[2,32,2560]{2,0,1:T(2,128)S(1)}, u32[]{:S(2)}, u32[]{:S(2)}) %all-to-all-start) | async-done | bytes 655392 | tf_op jit(solution)/shard_map/all_to_all | solution.py:137
  413.6 2.9 reshape.190
  416.5 5.2 %all-to-all-start.1 = ((f32[8,1,20480]{2,1,0:T(1,128)}), f32[8,1,20480]{2,1,0:T(1,128)S(1)}, u32[]{:S(2)}, u32[]{:S(2)}) async-start(f32[8,1,20480]{2,1,0:T(1,128)} %reshape.190), calls=%async_computation.3 | async-start | bytes 1310720 | tf_op jit(solution)/shard_map/all_to_all | solution.py:145
  421.9 16.7 %all-to-all-done.1 = f32[8,1,20480]{2,1,0:T(1,128)S(1)} async-done(((f32[8,1,20480]{2,1,0:T(1,128)}), f32[8,1,20480]{2,1,0:T(1,128)S(1)}, u32[]{:S(2)}, u32[]{:S(2)}) %all-to-all-start.1) | async-done | bytes 655392 | tf_op jit(solution)/shard_map/all_to_all | solution.py:145
  441.4 3.0 reshape.191
  450.7 2.8 fusion.59
  454.4 2.8 fusion.61
  457.2 2.8 fusion.18
  460.0 2.9 subtract_bitcast_fusion
  (117 shorter events, 50.5 us)
Async XLA Ops:
  6.5 92.9 %all-reduce.3.cloned.1.call-start = ((), (), s32[]{:S(2)}) async-start(), calls=%async_computation.4 | async-start | bytes 196608 | tf_op jit(solution)/shard_map/psum | solution.py:109
  6.5 11.1 %copy-start.4 = (f32[2,32,40,256]{3,2,1,0:T(8,128)S(1)}, f32[2,32,40,256]{3,2,1,0:T(8,128)}, u32[]{:S(2)}) copy-start(f32[2,32,40,256]{3,2,1,0:T(8,128)} %param.3) | copy-start | bytes 7864324
  17.7 5.5 %copy-start = (bf16[48,8,80,256]{3,1,2,0:T(8,128)(2,1)}, bf16[48,8,80,256]{3,1,2,0:T(8,128)(2,1)S(1)}, u32[]{:S(2)}) copy-start(bf16[48,8,80,256]{3,1,2,0:T(8,128)(2,1)S(1)} %copy.19) | copy-start | bytes 47185924
  26.4 117.3 %reduce-scatter.3.cloned.1.call-start = ((), (), s32[]{:S(2)}) async-start(), calls=%async_computation.5 | async-start | bytes 3276800 | tf_op jit(solution)/shard_map/reduce_scatter | solution.py:131
  109.9 102.5 %all-gather.2.cloned.1.call-start = ((), (), s32[]{:S(2)}) async-start(), calls=%async_computation.6 | async-start | bytes 1638400 | tf_op jit(solution)/shard_map/all_gather | solution.py:128
  143.6 48.3 %copy-start.2 = (f32[2,32,2560]{2,1,0:T(8,128)S(1)}, f32[2,32,2560]{2,1,0:T(8,128)}, u32[]{:S(2)}) copy-start(f32[2,32,2560]{2,1,0:T(8,128)} %reduce-scatter.3.cloned.1.call-done) | copy-start | bytes 1966084
  193.4 103.1 %all-reduce.5.cloned.1.call-start = ((), (), s32[]{:S(2)}) async-start(), calls=%async_computation.7 | async-start | bytes 196608 | tf_op jit(solution)/shard_map/psum | solution.py:109
  213.8 5.9 %copy-start.5 = (bf16[2,32,10240]{2,1,0:T(8,128)(2,1)S(1)}, bf16[2,32,10240]{2,1,0:T(8,128)(2,1)}, u32[]{:S(2)}) copy-start(bf16[2,32,10240]{2,1,0:T(8,128)(2,1)} %all-gather.2.cloned.1.call-done) | copy-start | bytes 3932164
  226.2 114.6 %reduce-scatter.5.cloned.1.call-start = ((), (), s32[]{:S(2)}) async-start(), calls=%async_computation.8 | async-start | bytes 3276800 | tf_op jit(solution)/shard_map/reduce_scatter | solution.py:131
  340.7 48.3 %copy-start.1 = (f32[2,32,2560]{2,1,0:T(8,128)S(1)}, f32[2,32,2560]{2,1,0:T(8,128)}, u32[]{:S(2)}) copy-start(f32[2,32,2560]{2,1,0:T(8,128)} %reduce-scatter.5.cloned.1.call-done) | copy-start | bytes 1966084
  391.1 14.2 %all-to-all-start = ((f32[2,32,2560]{2,0,1:T(2,128)}), f32[2,32,2560]{2,0,1:T(2,128)S(1)}, u32[]{:S(2)}, u32[]{:S(2)}) async-start(f32[2,32,2560]{2,0,1:T(2,128)} %copy.11), calls=%async_computation.2 | async-start | bytes 1310720 | tf_op jit(solution)/shard_map/all_to_all | solution.py:137
  416.5 22.2 %all-to-all-start.1 = ((f32[8,1,20480]{2,1,0:T(1,128)}), f32[8,1,20480]{2,1,0:T(1,128)S(1)}, u32[]{:S(2)}, u32[]{:S(2)}) async-start(f32[8,1,20480]{2,1,0:T(1,128)} %reshape.190), calls=%async_computation.3 | async-start | bytes 1310720 | tf_op jit(solution)/shard_map/all_to_all | solution.py:145
  448.5 5.0 %copy-start.3 = (f32[1,8,8,40,32]{4,2,3,1,0:T(8,128)S(1)}, f32[1,8,8,40,32]{4,2,3,1,0:T(8,128)}, u32[]{:S(2)}) copy-start(f32[1,8,8,40,32]{4,2,3,1,0:T(8,128)} %get-tuple-element.18) | copy-start | bytes 983044
Sparse Core Ops, SparseCore 0:
  26.5 72.8 all-reduce.2
  110.1 33.5 reduce-scatter.2
  193.5 18.8 all-gather.1
  226.3 70.1 all-reduce.4
  307.2 33.5 reduce-scatter.4
where the time goes:
time: 479 us; the launch traced here: 471 us
  waiting for transfers between devices  256 us (53%)
  blocking collectives  78.9 us (16%)
  matrix products  65.6 us (14%)
  local copies, waits for them, and re-layouts  31.2 us (7%)
  between operations  15.5 us (3%)
  other arithmetic  13.7 us (3%)
  starting transfers between devices  9.56 us (2%)
    psum x2, waiting for transfers between devices, pixel_sum(): return lax.psum(partial_value, 'pix')  143 us
    psum x2, blocking collectives, shards(): gram_total = lax.psum(gram_matrix(applied_share), ('elec', 'pix'))  78.9 us
    reduce_scatter x2, waiting for transfers between devices, shards(): lax.psum_scatter(covariance(waves, projected, mode_count), 'elec', scatte...  67.3 us
    unnamed x18, local copies, waits for them, and re-layouts  19.7 us
    all_gather x1, waiting for transfers between devices, shards(): lax.all_gather(share_low, 'elec', axis=2, tiled=True)  18.8 us
    all_to_all x1, waiting for transfers between devices, shards(): lax.all_to_all(spectrum, 'pix', split_axis=3, concat_axis=2, tiled=True)  16.7 us
    dot_general x2, matrix products, covariance(): lax.dot_general(both, waves, (((0,), (0,)), ((), ())), preferred_element_...  14.1 us
    all_to_all x1, waiting for transfers between devices, shards(): lax.all_to_all(share_modes, 'elec', split_axis=1, concat_axis=2, tiled=True)  9.93 us
  transfers between devices with their start and end apart: 7, of which 7 were waited for; matrix products, arithmetic and copies ran while one was open for 0% of the time, Pallas kernels for 0%

commit v1 on v0

v1 whole, which is shorter than its diff:
```python
import functools
import math

import jax
import jax.numpy as jnp
import numpy as np
from jax import lax
from jax.experimental import pallas as pl
from jax.experimental.pallas import tpu as pltpu
from jax.sharding import PartitionSpec as P

ITERS = 2
NS_STEPS = 8

HIGH = lax.Precision.HIGHEST
MESH = pl.DeviceIdType.MESH


def greet(peers, axis):
    barrier = pltpu.get_barrier_semaphore()
    for peer in peers:
        pl.semaphore_signal(barrier, inc=1, device_id={axis: peer}, device_id_type=MESH)
    pl.semaphore_wait(barrier, len(peers))


def remote(src, dst, send_sem, recv_sem, axis, peer):
    return pltpu.make_async_remote_copy(
        src_ref=src,
        dst_ref=dst,
        send_sem=send_sem,
        recv_sem=recv_sem,
        device_id={axis: peer},
        device_id_type=MESH,
    )


def sum_kernel(n, axis, x_ref, out_ref, held, send_a, recv_a, send_b, recv_b):
    me = lax.axis_index(axis)
    peers = [lax.rem(me + d, n) for d in range(1, n)]
    greet(peers, axis)
    scatter = []
    for d in range(1, n):
        copy = remote(
            x_ref.at[peers[d - 1]], held.at[d], send_a.at[d], recv_a.at[d], axis, peers[d - 1]
        )
        copy.start()
        scatter.append(copy)
    total = x_ref[me]
    for d in range(1, n):
        scatter[d - 1].wait_recv()
        total = total + held[d]
    out_ref[me] = total
    gather = []
    for d in range(1, n):
        copy = remote(
            out_ref.at[me], out_ref.at[me], send_b.at[d], recv_b.at[d], axis, peers[d - 1]
        )
        copy.start()
        gather.append(copy)
    for d in range(1, n):
        source = lax.rem(me + n - d, n)
        remote(
            out_ref.at[source], out_ref.at[source], send_b.at[d], recv_b.at[d], axis, source
        ).wait_recv()
    for copy in scatter + gather:
        copy.wait_send()


def axis_sum(value, axis, collective_id):
    n = lax.axis_size(axis)
    rows, width = value.shape
    chunk = rows // n
    shape = (n, chunk, width)
    vmem = pl.BlockSpec(memory_space=pltpu.VMEM)
    dma = pltpu.SemaphoreType.DMA
    total = pl.pallas_call(
        functools.partial(sum_kernel, n, axis),
        out_shape=jax.ShapeDtypeStruct(shape, jnp.float32),
        in_specs=[vmem],
        out_specs=vmem,
        scratch_shapes=[pltpu.VMEM(shape, jnp.float32)] + [dma((n,))] * 4,
        compiler_params=pltpu.CompilerParams(collective_id=collective_id, has_side_effects=True),
        name=f"sum_{axis}_{collective_id}",
    )(value.reshape(shape))
    return total.reshape(rows, width)


def group_kernel(n, pieces, x_ref, out_ref, pair, half, far, sa, ra, sb, rb, sc, rc, sd, rd, se, re):
    me = lax.axis_index("elec")
    core = lax.rem(me, 2)
    chip = me // 2
    chips = n // 2
    partner = chip * 2 + 1 - core
    width = x_ref.shape[2] // pieces
    others = [lax.rem(chip + d, chips) for d in range(1, chips)]
    seats = [other * 2 + core for other in others]
    greet([partner] + seats, "elec")

    def part(ref, index, piece):
        return ref.at[index, :, pl.ds(piece * width, width)]

    def cut(piece):
        return pl.ds(piece * width, width)

    order = others + [chip]
    started = []
    first = {}
    for piece in range(pieces):
        for d, other in enumerate(order):
            slot = d * pieces + piece
            copy = remote(
                part(x_ref, other * 2 + 1 - core, piece),
                part(pair, d, piece),
                sa.at[slot],
                ra.at[slot],
                "elec",
                partner,
            )
            copy.start()
            started.append(copy)
            first[d, piece] = copy
    second = {}
    for piece in range(pieces):
        for d in range(chips - 1):
            slot = d * pieces + piece
            first[d, piece].wait_recv()
            half[d, :, cut(piece)] = (
                x_ref[seats[d], :, cut(piece)].astype(jnp.float32)
                + pair[d, :, cut(piece)].astype(jnp.float32)
            ).astype(jnp.bfloat16)
            copy = remote(
                part(half, d, piece), part(far, d, piece), sb.at[slot], rb.at[slot], "elec", seats[d]
            )
            copy.start()
            started.append(copy)
            second[d, piece] = copy
    for piece in range(pieces):
        first[chips - 1, piece].wait_recv()
        total = x_ref[me, :, cut(piece)].astype(jnp.float32) + pair[
            chips - 1, :, cut(piece)
        ].astype(jnp.float32)
        for d in range(chips - 1):
            second[d, piece].wait_recv()
            total = total + far[d, :, cut(piece)].astype(jnp.float32)
        out_ref[me, :, cut(piece)] = total.astype(jnp.bfloat16)
        for d in range(chips - 1):
            slot = d * pieces + piece
            copy = remote(
                part(out_ref, me, piece),
                part(out_ref, me, piece),
                sc.at[slot],
                rc.at[slot],
                "elec",
                seats[d],
            )
            copy.start()
            started.append(copy)
        copy = remote(
            part(out_ref, me, piece),
            part(out_ref, me, piece),
            sd.at[piece],
            rd.at[piece],
            "elec",
            partner,
        )
        copy.start()
        started.append(copy)
    for piece in range(pieces):
        for d in range(chips - 1):
            slot = d * pieces + piece
            source = lax.rem(chip + chips - 1 - d, chips) * 2 + core
            block = part(out_ref, source, piece)
            remote(block, block, sc.at[slot], rc.at[slot], "elec", source).wait_recv()
            copy = remote(block, block, se.at[slot], re.at[slot], "elec", partner)
            copy.start()
            started.append(copy)
    for piece in range(pieces):
        block = part(out_ref, partner, piece)
        remote(block, block, sd.at[piece], rd.at[piece], "elec", partner).wait_recv()
        for d in range(chips - 1):
            slot = d * pieces + piece
            source = lax.rem(chip + chips - 1 - d, chips) * 2 + 1 - core
            block = part(out_ref, source, piece)
            remote(block, block, se.at[slot], re.at[slot], "elec", partner).wait_recv()
    for copy in started:
        copy.wait_send()


def group_sum(value, collective_id):
    n = lax.axis_size("elec")
    rows, width = value.shape
    pieces = next(count for count in (4, 2, 1) if width % (128 * count) == 0)
    chips = n // 2
    chunk = rows // n
    shape = (n, chunk, width)
    vmem = pl.BlockSpec(memory_space=pltpu.VMEM)
    dma = pltpu.SemaphoreType.DMA
    slots = chips * pieces
    total = pl.pallas_call(
        functools.partial(group_kernel, n, pieces),
        out_shape=jax.ShapeDtypeStruct(shape, jnp.bfloat16),
        in_specs=[vmem],
        out_specs=vmem,
        scratch_shapes=[
            pltpu.VMEM((chips, chunk, width), jnp.bfloat16),
            pltpu.VMEM((chips, chunk, width), jnp.bfloat16),
            pltpu.VMEM((chips, chunk, width), jnp.bfloat16),
        ]
        + [dma((slots,))] * 10,
        compiler_params=pltpu.CompilerParams(collective_id=collective_id, has_side_effects=True),
        name=f"group_{collective_id}",
    )(value.reshape(shape))
    return total.reshape(rows, width)


def swap_kernel(n, axis, x_ref, out_ref, own_sem, send, recv):
    me = lax.axis_index(axis)
    peers = [lax.rem(me + d, n) for d in range(1, n)]
    greet(peers, axis)
    copies = []
    for d in range(1, n):
        copy = remote(
            x_ref.at[peers[d - 1]], out_ref.at[me], send.at[d], recv.at[d], axis, peers[d - 1]
        )
        copy.start()
        copies.append(copy)
    own = pltpu.make_async_copy(x_ref.at[me], out_ref.at[me], own_sem)
    own.start()
    own.wait()
    for d in range(1, n):
        source = lax.rem(me + n - d, n)
        remote(
            x_ref.at[source], out_ref.at[source], send.at[d], recv.at[d], axis, source
        ).wait_recv()
    for copy in copies:
        copy.wait_send()


def swap(value, axis, collective_id):
    n = lax.axis_size(axis)
    vmem = pl.BlockSpec(memory_space=pltpu.VMEM)
    dma = pltpu.SemaphoreType.DMA
    return pl.pallas_call(
        functools.partial(swap_kernel, n, axis),
        out_shape=jax.ShapeDtypeStruct(value.shape, value.dtype),
        in_specs=[vmem],
        out_specs=vmem,
        scratch_shapes=[dma, dma((n,)), dma((n,))],
        compiler_params=pltpu.CompilerParams(collective_id=collective_id, has_side_effects=True),
        name=f"swap_{axis}",
    )(value)


def project(wave_re, wave_im, stacked):
    half = stacked.shape[0] // 2
    swapped = jnp.concatenate([-stacked[half:], stacked[:half]], axis=0)
    contract = (((1,), (1,)), ((), ()))
    real_side = lax.dot_general(stacked, wave_re, contract, preferred_element_type=jnp.float32)
    imag_side = lax.dot_general(swapped, wave_im, contract, preferred_element_type=jnp.float32)
    return real_side + imag_side


def covariance(waves, projected, mode_count):
    pixels = waves.shape[1] // 2
    width = projected.shape[0]
    upper = lax.reduce_precision(projected, 8, 7)
    lower = (projected - upper).astype(jnp.bfloat16)
    both = jnp.concatenate([upper.astype(jnp.bfloat16), lower], axis=0)
    stacked = lax.dot_general(
        both, waves, (((1,), (0,)), ((), ())), preferred_element_type=jnp.float32
    )
    blocks = stacked[:width] + stacked[width:]
    real_part = blocks[:mode_count, :pixels] + blocks[mode_count:, pixels:]
    imag_part = blocks[mode_count:, :pixels] - blocks[:mode_count, pixels:]
    return jnp.concatenate([real_part, imag_part], axis=0)


def gram_matrix(flat):
    return lax.dot_general(flat, flat, (((1,), (1,)), ((), ())), preferred_element_type=jnp.float32)


def embed(gram_raw, mode_count):
    gram_re = gram_raw[:mode_count, :mode_count] + gram_raw[mode_count:, mode_count:]
    gram_im = gram_raw[:mode_count, mode_count:] - gram_raw[mode_count:, :mode_count]
    return jnp.concatenate(
        [jnp.concatenate([gram_re, -gram_im], 1), jnp.concatenate([gram_im, gram_re], 1)], 0
    )


def newton_schulz(scaled):
    identity = jnp.eye(scaled.shape[0], dtype=scaled.dtype)
    inverse_root = identity
    for step in range(NS_STEPS):
        product = scaled if step == 0 else jnp.dot(inverse_root, scaled, precision=HIGH)
        correction = 1.5 * identity - 0.5 * product
        if step == 0:
            inverse_root = correction
        else:
            inverse_root = jnp.dot(correction, inverse_root, precision=HIGH)
        if step + 1 < NS_STEPS:
            scaled = jnp.dot(scaled, correction, precision=HIGH)
    return inverse_root


def dft_table(length):
    index = np.arange(length, dtype=np.int64)
    angle = 2.0 * np.pi / length * (index[:, None] * index[None, :] % length)
    return np.cos(angle).astype(np.float32), -np.sin(angle).astype(np.float32)


def split(table):
    upper = table.astype(jnp.bfloat16)
    lower = (table - upper.astype(np.float32)).astype(jnp.bfloat16)
    return upper, lower


def chirp_phase(row_pos, col_pos, row_total, col_total, factor):
    row_term = (row_pos - row_total / 2.0) ** 2 / row_total
    col_term = (col_pos - col_total / 2.0) ** 2 / col_total
    angle = math.pi * factor * (row_term[:, None] + col_term[None, :])
    return (jnp.cos(angle), jnp.sin(angle))


def column_section(field, row_pos, row_total, col_total, pix_count):
    share, rows_dev = field.shape[1], field.shape[2]
    col_pos = jnp.arange(col_total, dtype=jnp.float32)
    chirp_re, chirp_im = chirp_phase(row_pos, col_pos, row_total, col_total, 0.5)
    launch_re = chirp_re * field[0] - chirp_im * field[1]
    launch_im = chirp_re * field[1] + chirp_im * field[0]
    table_re, table_im = dft_table(col_total)
    both = np.concatenate([table_re, table_im], axis=1)
    launch = jnp.stack([launch_re, launch_im]).reshape(2 * share * rows_dev, col_total)
    wide = jnp.dot(launch, jnp.asarray(both), precision=lax.Precision.HIGH)
    wide = wide.reshape(2, share, rows_dev, 2, pix_count, col_total // pix_count)
    spec_re = wide[0, :, :, 0] - wide[1, :, :, 1]
    spec_im = wide[0, :, :, 1] + wide[1, :, :, 0]
    spec = jnp.stack([spec_re, spec_im]).astype(jnp.bfloat16)
    return spec.transpose(3, 2, 0, 1, 4).reshape(pix_count, rows_dev, -1)


def row_section(spectrum, share, col_pos, row_total, col_total):
    width = col_pos.shape[0]
    table_re, table_im = dft_table(row_total)
    upper, lower = split(np.concatenate([table_re, table_im], axis=0))
    tables = np.concatenate([upper, lower], axis=0)
    wide = jnp.dot(jnp.asarray(tables), spectrum, preferred_element_type=jnp.float32)
    wide = wide[: 2 * row_total] + wide[2 * row_total :]
    half = share * width
    out_re = wide[:row_total, :half] - wide[row_total:, half:]
    out_im = wide[:row_total, half:] + wide[row_total:, :half]
    row_pos = jnp.arange(row_total, dtype=jnp.float32)
    chirp_re, chirp_im = chirp_phase(row_pos, col_pos, row_total, col_total, 0.25)
    out_re = out_re.reshape(row_total, share, width).transpose(1, 0, 2)
    out_im = out_im.reshape(row_total, share, width).transpose(1, 0, 2)
    return jnp.stack([chirp_re * out_re - chirp_im * out_im, chirp_re * out_im + chirp_im * out_re])


def shards(wavefronts, trial_modes):
    electrons_dev, _, rows_dev, cols = wavefronts.shape
    mode_count = trial_modes.shape[1]
    pixels = rows_dev * cols
    groups = lax.axis_size("elec")
    share = mode_count // groups
    waves = wavefronts.reshape(electrons_dev, 2 * pixels)
    wave_re = waves[:, :pixels]
    wave_im = waves[:, pixels:]
    low = trial_modes.astype(jnp.bfloat16).reshape(2 * mode_count, pixels)

    projected = axis_sum(project(wave_re, wave_im, low), "pix", 1)
    applied = group_sum(covariance(waves, projected, mode_count).astype(jnp.bfloat16), 2)

    turn = None
    for iteration in range(1, ITERS):
        gram_part = jnp.pad(gram_matrix(applied), ((0, 0), (0, -2 * mode_count % 128)))
        payload = jnp.concatenate([project(wave_re, wave_im, applied), gram_part], axis=1)
        summed = axis_sum(payload, "pix", 2 * iteration + 1)
        gram_raw = summed[:, electrons_dev : electrons_dev + 2 * mode_count]
        if turn is not None:
            gram_raw = jnp.dot(jnp.dot(turn, gram_raw, precision=HIGH), turn.T, precision=HIGH)
        embedded = embed(gram_raw, mode_count)
        trace_value = jnp.trace(embedded)
        step_turn = newton_schulz(embedded / trace_value).T
        turn = step_turn if turn is None else jnp.dot(step_turn, turn, precision=HIGH)
        projected = summed[:, :electrons_dev] * (1.0 / jnp.sqrt(trace_value))
        applied = group_sum(
            covariance(waves, projected, mode_count).astype(jnp.bfloat16), 2 * iteration + 2
        )
    gram_part = jnp.pad(gram_matrix(applied), ((0, 0), (0, -2 * mode_count % 128)))
    gram_raw = axis_sum(gram_part, "pix", 2 * ITERS + 1)[:, : 2 * mode_count]
    if turn is not None:
        gram_raw = jnp.dot(jnp.dot(turn, gram_raw, precision=HIGH), turn.T, precision=HIGH)
    embedded = embed(gram_raw, mode_count)
    trace_value = jnp.trace(embedded)
    last = (newton_schulz(embedded / trace_value) / jnp.sqrt(trace_value)).T
    turn = last if turn is None else jnp.dot(last, turn, precision=HIGH)
    mine = lax.dynamic_slice_in_dim(
        turn.reshape(2, mode_count, 2 * mode_count), lax.axis_index("elec") * share, share, axis=1
    ).reshape(2 * share, 2 * mode_count)
    mine_upper = lax.reduce_precision(mine, 8, 7)
    mine_lower = (mine - mine_upper).astype(jnp.bfloat16)
    field = jnp.dot(
        mine_upper.astype(jnp.bfloat16), applied, preferred_element_type=jnp.float32
    ) + jnp.dot(mine_lower, applied, preferred_element_type=jnp.float32)
    field = field.reshape(2, share, rows_dev, cols)

    pix_count = lax.axis_size("pix")
    row_total = rows_dev * pix_count
    row_pos = (lax.axis_index("pix") * rows_dev + jnp.arange(rows_dev, dtype=jnp.int32)).astype(
        jnp.float32
    )
    spectrum = column_section(field, row_pos, row_total, cols, pix_count)
    column_block = swap(spectrum, "pix", 2 * ITERS + 2).reshape(row_total, -1)
    width = cols // pix_count
    col_pos = (lax.axis_index("pix") * width + jnp.arange(width, dtype=jnp.int32)).astype(
        jnp.float32
    )
    return row_section(column_block, share, col_pos, row_total, cols)


def solution(mesh):
    in_specs = (P("elec", None, "pix", None), P(None, None, "pix", None))
    out_specs = P(None, "elec", None, "pix")
    return jax.shard_map(shards, mesh=mesh, in_specs=in_specs, out_specs=out_specs, check_vma=False)
```

time: 479 us -> 180 us (0.38); the launches traced: 471 us -> 179 us
  waiting for transfers between devices: 256 us -> 0 us
  Pallas kernels: 0 us -> 94.6 us
  blocking collectives: 78.9 us -> 0 us
  matrix products: 65.6 us -> 51.4 us
  between operations: 15.5 us -> 2.15 us
  local copies, waits for them, and re-layouts: 31.2 us -> 18.5 us
  starting transfers between devices: 9.56 us -> 0 us
    psum x2 -> x0, waiting for transfers between devices: 143 us -> none  [pixel_sum(): return lax.psum(partial_value, 'pix')]
    pallas_call x0 -> x6, Pallas kernels: none -> 94.6 us  [the longest x2 43.6 us: group_sum(): pl.pallas_call(functools.partial(group_kernel, n, pieces), out_shape=jax....]
    psum x2 -> x0, blocking collectives: 78.9 us -> none  [shards(): gram_total = lax.psum(gram_matrix(applied_share), ('elec', 'pix'))]
    reduce_scatter x2 -> x0, waiting for transfers between devices: 67.3 us -> none  [shards(): lax.psum_scatter(covariance(waves, projected, mode_count), 'elec', scatte...]
    all_to_all x2 -> x0, waiting for transfers between devices: 26.6 us -> none  [the longest x1 16.7 us: shards(): lax.all_to_all(spectrum, 'pix', split_axis=3, concat_axis=2, tiled=True)]
    all_gather x1 -> x0, waiting for transfers between devices: 18.8 us -> none  [shards(): lax.all_gather(share_low, 'elec', axis=2, tiled=True)]
    dot_general x64 -> x57, matrix products: 65.6 us -> 51.4 us  [the longest x2 14.5 us: covariance(): lax.dot_general(both, waves, (((1,), (0,)), ((), ())), preferred_element_...]
    all_to_all x2 -> x0, starting transfers between devices: 9.17 us -> none  [the longest x1 5.16 us: shards(): lax.all_to_all(spectrum, 'pix', split_axis=3, concat_axis=2, tiled=True)]
  transfers between devices with their start and end apart: 7 -> 0, of which waited for: 7 -> 0; matrix products, arithmetic and copies ran while one was open for 0% -> 0% of each run, Pallas kernels for 0% -> 0%
where the time goes in v1:
time: 180 us; the launch traced here: 179 us
  Pallas kernels  94.6 us (53%)
  matrix products  51.4 us (29%)
  local copies, waits for them, and re-layouts  18.5 us (10%)
  other arithmetic  12.1 us (7%)
  between operations  2.15 us (1%)
    pallas_call x2, Pallas kernels, group_sum(): pl.pallas_call(functools.partial(group_kernel, n, pieces), out_shape=jax....  43.6 us
    pallas_call x3, Pallas kernels, axis_sum(): pl.pallas_call(functools.partial(sum_kernel, n, axis), out_shape=jax.Shap...  42.3 us
    dot_general x2, matrix products, covariance(): lax.dot_general(both, waves, (((1,), (0,)), ((), ())), preferred_element_...  14.5 us
    unnamed x18, local copies, waits for them, and re-layouts  14.3 us
    dot_general x2, matrix products, project(): lax.dot_general(stacked, wave_re, contract, preferred_element_type=jnp.fl...  9 us
    pallas_call x1, Pallas kernels, swap(): pl.pallas_call(functools.partial(swap_kernel, n, axis), out_shape=jax.Sha...  8.66 us
    dot_general x2, matrix products, project(): lax.dot_general(swapped, wave_im, contract, preferred_element_type=jnp.fl...  8.38 us
    dot_general x14, matrix products, newton_schulz(): scaled = jnp.dot(scaled, correction, precision=HIGH)  3.81 us

profile of v1, /device:TPU:0, one launch (start us, length us, event | category | flops | bytes accessed | tf_op | source)
XLA Modules:
  0.0 178.8 jit_solution(8994905964596830180)
XLA Ops:
  0.0 11.1 %copy.30 = bf16[48,8,80,256]{3,1,2,0:T(8,128)(2,1)S(1)} copy(bf16[48,8,80,256]{3,2,1,0:T(8,128)(2,1)} %bitcast.184) | data formatting | bytes 31457280
  11.6 2.5 %fusion.2 = f32[64,384]{1,0:T(8,128)S(1)} fusion(bf16[384,20480]{1,0:T(8,128)(2,1)S(1)} %bitcast.173, bf16[32,10240]{1,0:T(8,128)(2,1)S(1)} %bitcast.201, bf16[32,10240]{1,0:T(8,128)(2,1)S(1)} %bitcast.200), kind=kOutput, calls=%fused_computation.3 | convolution fusion | flops 505937920 | bytes 9273344 | tf_op jit(solution)/shard_map/dot_general | solution.py:259
  14.4 2.2 %copy-done = bf16[48,8,80,256]{3,1,2,0:T(8,128)(2,1)} copy-done((bf16[48,8,80,256]{3,1,2,0:T(8,128)(2,1)}, bf16[48,8,80,256]{3,1,2,0:T(8,128)(2,1)S(1)}, u32[]{:S(2)}) %copy-start) | copy-done | bytes 15728664
  16.6 3.2 %fusion.21.x_ref = f32[8,8,384]{2,1,0:T(8,128)} fusion(f32[64,384]{1,0:T(8,128)S(1)} %fusion.2, bf16[64,10240]{1,0:T(8,128)(2,1)S(1)} %bitcast.192, bf16[384,20480]{1,0:T(8,128)(2,1)S(1)} %bitcast.174), kind=kOutput, calls=%fused_computation.29 | convolution fusion | flops 503341056 | bytes 9371648 | tf_op jit(solution)/shard_map/dot_general | solution.py:258
  19.8 16.6 %sum_pix_1.1 = f32[8,8,384]{2,1,0:T(8,128)} custom-call(f32[8,8,384]{2,1,0:T(8,128)} %fusion.21.x_ref), custom_call_target="tpu_custom_call" | custom-call | tf_op jit(solution)/shard_map/sum_pix_1/pallas_call | solution.py:76
  37.3 7.2 %fusion.52 = f32[128,20480]{1,0:T(8,128)S(1)} fusion(bf16[384,20480]{1,0:T(8,128)(2,1)} %bitcast.175, bf16[64,384]{1,0:T(8,128)(2,1)S(1)} %get-tuple-element.29, bf16[64,384]{1,0:T(8,128)(2,1)S(1)} %get-tuple-element.28), kind=kOutput, calls=%fused_computation.94 | convolution fusion | flops 2013462528 | bytes 26312704 | tf_op jit(solution)/shard_map/dot_general | solution.py:269
  45.3 1.2 pad_maximum_fusion
  46.5 22.3 %group_2.1 = bf16[4,16,10240]{2,1,0:T(8,128)(2,1)} custom-call(bf16[4,16,10240]{2,1,0:T(8,128)(2,1)} %bitcast.186), custom_call_target="tpu_custom_call" | custom-call | tf_op jit(solution)/shard_map/group_2/pallas_call | solution.py:199
  68.7 1.4 slice_negate_fusion.1
  70.1 5.9 %fusion = f32[64,384]{1,0:T(8,128)S(1)} fusion(bf16[384,20480]{1,0:T(8,128)(2,1)} %bitcast.176, bf16[32,10240]{1,0:T(8,128)(2,1)S(1)} %bitcast.199, bf16[32,10240]{1,0:T(8,128)(2,1)S(1)} %bitcast.198), kind=kOutput, calls=%fused_computation.1 | convolution fusion | flops 505937920 | bytes 9273344 | tf_op jit(solution)/shard_map/dot_general | solution.py:259
  76.0 5.8 %fusion.24 = f32[64,384]{1,0:T(8,128)S(1)} fusion(f32[64,384]{1,0:T(8,128)S(1)} %fusion, bf16[64,10240]{1,0:T(8,128)(2,1)S(1)} %bitcast.182, bf16[384,20480]{1,0:T(8,128)(2,1)} %bitcast.177), kind=kOutput, calls=%fused_computation.30 | convolution fusion | flops 503341056 | bytes 9371648 | tf_op jit(solution)/shard_map/dot_general | solution.py:258
  83.0 12.9 %sum_pix_3.1 = f32[8,8,512]{2,1,0:T(8,128)} custom-call(f32[8,8,512]{2,1,0:T(8,128)} %fusion.49.x_ref), custom_call_target="tpu_custom_call" | custom-call | tf_op jit(solution)/shard_map/sum_pix_3/pallas_call | solution.py:76
  103.9 7.3 %fusion.56 = f32[128,20480]{1,0:T(8,128)S(1)} fusion(bf16[384,20480]{1,0:T(8,128)(2,1)} %bitcast.178, bf16[64,384]{1,0:T(8,128)(2,1)S(1)} %get-tuple-element.26, bf16[64,384]{1,0:T(8,128)(2,1)S(1)} %get-tuple-element.25), kind=kOutput, calls=%fused_computation.98 | convolution fusion | flops 2013462528 | bytes 26312704 | tf_op jit(solution)/shard_map/dot_general | solution.py:269
  111.9 1.2 pad_maximum_fusion.1
  113.1 21.4 %group_4.1 = bf16[4,16,10240]{2,1,0:T(8,128)(2,1)} custom-call(bf16[4,16,10240]{2,1,0:T(8,128)(2,1)} %bitcast.187), custom_call_target="tpu_custom_call" | custom-call | tf_op jit(solution)/shard_map/group_4/pallas_call | solution.py:199
  134.4 2.2 %fusion.135 = f32[64,64]{1,0:T(8,128)S(1)} fusion(bf16[64,10240]{1,0:T(8,128)(2,1)} %bitcast.179), kind=kOutput, calls=%fused_computation.195 | convolution fusion | flops 83886080 | bytes 1327104 | tf_op jit(solution)/shard_map/dot_general | solution.py:279
  137.3 12.8 %sum_pix_5.1 = f32[8,8,128]{2,1,0:T(8,128)} custom-call(f32[8,8,128]{2,1,0:T(8,128)} %pad_bitcast_fusion.x_ref), custom_call_target="tpu_custom_call" | custom-call | tf_op jit(solution)/shard_map/sum_pix_5/pallas_call | solution.py:76
  150.1 1.0 fusion.64
  152.0 1.0 fusion.67
  160.5 1.9 %fusion.44 = f32[2,8,40,2,8,32]{2,5,4,3,1,0:T(8,128)S(1)} fusion(f32[2,8,32,256,1,1]{3,2,1,0,5,4:T(8,128)S(1)} %copy-done.6, f32[1,8,40,256]{3,2,1,0:T(8,128)S(1)} %get-tuple-element.22, f32[1,8,40,256]{3,2,1,0:T(8,128)S(1)} %get-tuple-element.21), kind=kOutput, calls=%fused_computation.70 | convolution fusion | flops 503480320 | bytes 2490368 | tf_op jit(solution)/shard_map/dot_general | solution.py:333
  163.1 1.2 copy.22
  164.3 2.0 %reshape.305.x_ref = bf16[8,40,512]{2,1,0:T(8,128)(2,1)} reshape(bf16[8,40,2,8,32]{4,3,2,1,0:T(8,128)(2,1)S(1)} %copy.22) | data formatting | bytes 655360 | tf_op jit(solution)/shard_map/reshape | solution.py:338
  166.3 8.7 %swap_pix.1 = bf16[8,40,512]{2,1,0:T(8,128)(2,1)} custom-call(bf16[8,40,512]{2,1,0:T(8,128)(2,1)} %reshape.305.x_ref), custom_call_target="tpu_custom_call" | custom-call | tf_op jit(solution)/shard_map/swap_pix/pallas_call | solution.py:243
  175.0 1.8 %fusion.149 = f32[1280,512]{1,0:T(8,128)S(1)} fusion(bf16[1280,320]{1,0:T(8,128)(2,1)S(1)} %copy-done.4, bf16[320,512]{1,0:T(8,128)(2,1)} %bitcast.195), kind=kOutput, calls=%fused_computation.209 | convolution fusion | flops 419430400 | bytes 3768320 | tf_op jit(solution)/shard_map/dot_general | solution.py:346
  (93 shorter events, 22.2 us)
Async XLA Ops:
  0.0 11.1 %copy-start.3 = (f32[2,32,40,256]{3,2,1,0:T(8,128)S(1)}, f32[2,32,40,256]{3,2,1,0:T(8,128)}, u32[]{:S(2)}) copy-start(f32[2,32,40,256]{3,2,1,0:T(8,128)} %param.5) | copy-start | bytes 7864324
  11.1 5.5 %copy-start = (bf16[48,8,80,256]{3,1,2,0:T(8,128)(2,1)}, bf16[48,8,80,256]{3,1,2,0:T(8,128)(2,1)S(1)}, u32[]{:S(2)}) copy-start(bf16[48,8,80,256]{3,1,2,0:T(8,128)(2,1)S(1)} %copy.30) | copy-start | bytes 47185924
  70.1 5.9 %copy-start.2 = (bf16[4,16,10240]{2,1,0:T(8,128)(2,1)S(1)}, bf16[4,16,10240]{2,1,0:T(8,128)(2,1)}, u32[]{:S(2)}) copy-start(bf16[4,16,10240]{2,1,0:T(8,128)(2,1)} %group_2.1) | copy-start | bytes 3932164
  96.7 7.1 %copy-start.5 = (f32[8,8,512]{2,1,0:T(8,128)S(1)}, f32[8,8,512]{2,1,0:T(8,128)}, u32[]{:S(2)}) copy-start(f32[8,8,512]{2,1,0:T(8,128)} %sum_pix_3.1) | copy-start | bytes 393220
  152.0 6.8 %copy-start.1 = (bf16[4,16,10240]{2,1,0:T(8,128)(2,1)S(1)}, bf16[4,16,10240]{2,1,0:T(8,128)(2,1)}, u32[]{:S(2)}) copy-start(bf16[4,16,10240]{2,1,0:T(8,128)(2,1)} %group_4.1) | copy-start | bytes 3932164
  159.4 1.0 copy-start.6
  164.3 10.7 %copy-start.4 = (bf16[1280,320]{1,0:T(8,128)(2,1)S(1)}, bf16[1280,320]{1,0:T(8,128)(2,1)}, u32[]{:S(2)}) copy-start(bf16[1280,320]{1,0:T(8,128)(2,1)} %constant.59.clone) | copy-start | bytes 2457604

commit v2 on v1

v2 whole, which is shorter than its diff:
```python
import functools
import math

import jax
import jax.numpy as jnp
import numpy as np
from jax import lax
from jax.experimental import pallas as pl
from jax.experimental.pallas import tpu as pltpu
from jax.sharding import PartitionSpec as P

NS_STEPS = 8

HIGH = lax.Precision.HIGHEST
MESH = pl.DeviceIdType.MESH


def greet(*groups):
    barrier = pltpu.get_barrier_semaphore()
    for axis, peers in groups:
        for peer in peers:
            pl.semaphore_signal(barrier, inc=1, device_id={axis: peer}, device_id_type=MESH)
    pl.semaphore_wait(barrier, sum(len(peers) for _, peers in groups))


def remote(src, dst, send_sem, recv_sem, axis, peer):
    return pltpu.make_async_remote_copy(
        src_ref=src,
        dst_ref=dst,
        send_sem=send_sem,
        recv_sem=recv_sem,
        device_id={axis: peer},
        device_id_type=MESH,
    )


NT = (((1,), (1,)), ((), ()))
NN = (((1,), (0,)), ((), ()))


def dot(left, right, dims):
    return lax.dot_general(left, right, dims, preferred_element_type=jnp.float32)


def scatter_gather(n, peers, x_ref, held, out_ref, send_a, recv_a, send_b, recv_b):
    me = lax.axis_index("pix")
    started = []
    scatter = []
    for d in range(1, n):
        peer = peers[d - 1]
        copy = remote(x_ref.at[peer], held.at[d], send_a.at[d], recv_a.at[d], "pix", peer)
        copy.start()
        scatter.append(copy)
    total = x_ref[me]
    for d in range(1, n):
        scatter[d - 1].wait_recv()
        total = total + held[d]
    out_ref[me] = total
    for d in range(1, n):
        copy = remote(
            out_ref.at[me], out_ref.at[me], send_b.at[d], recv_b.at[d], "pix", peers[d - 1]
        )
        copy.start()
        started.append(copy)
    for d in range(1, n):
        source = lax.rem(me + n - d, n)
        block = out_ref.at[source]
        remote(block, block, send_b.at[d], recv_b.at[d], "pix", source).wait_recv()
    return scatter + started


def core_kernel(
    np_, ne, pieces, sub, electrons, modes,
    waves_ref, part_ref,
    applied_ref, gram_ref, turn_ref,
    rows_a, both_ref, cut_ref, emb_ref,
    held_a, total_a, pay_ref, held_b, total_b,
    x_ref, pair, half, far, first_ref, gram_in,
    ps, es, gs,
):
    pixels = waves_ref.shape[1] // 2
    order = 2 * modes
    chunk = order // ne
    depth = order // np_
    width = pixels // pieces
    me_p = lax.axis_index("pix")
    peers = [lax.rem(me_p + d, np_) for d in range(1, np_)]
    me = lax.axis_index("elec")
    core = lax.rem(me, 2)
    chip = me // 2
    chips = ne // 2
    partner = chip * 2 + 1 - core
    others = [lax.rem(chip + d, chips) for d in range(1, chips)]
    seats = [other * 2 + core for other in others]
    sources = [lax.rem(chip + chips - d, chips) for d in range(1, chips)]
    greet(("pix", peers), ("elec", [partner] + seats))
    started = scatter_gather(
        np_, peers, part_ref, held_a, total_a, ps.at[0], ps.at[1], ps.at[2], ps.at[3]
    )
    for j in range(np_):
        rows_a[pl.ds(j * depth, depth), 0:electrons] = total_a[j]

    def split_rows(value):
        upper = value.astype(jnp.bfloat16)
        both_ref[0:order, :] = upper
        both_ref[order : 2 * order, :] = (value - upper.astype(jnp.float32)).astype(jnp.bfloat16)

    def part(ref, lead, piece):
        return ref.at[lead, :, pl.ds(piece * width, width)]

    def cut(piece):
        return pl.ds(piece * width, width)

    def round_trip(turn, gathered, finish, beside):
        sa, ra, sb, rb, sc, rc, sd, rd, se, re = [es.at[10 * turn + i] for i in range(10)]
        first, second = {}, {}

        def compute(piece):
            def body(step, carry):
                start = pl.multiple_of(piece * width + step * sub, 128)
                both = both_ref[...]
                from_re = dot(both, waves_ref[:, pl.ds(start, sub)], NN)
                from_im = dot(both, waves_ref[:, pl.ds(pl.multiple_of(pixels + start, 128), sub)], NN)
                from_re = from_re[:order] + from_re[order:]
                from_im = from_im[:order] + from_im[order:]
                real = from_re[:modes] + from_im[modes:]
                imag = from_re[modes:] - from_im[:modes]
                if chunk % 16 == 0:
                    whole = jnp.concatenate([real, imag], axis=0).astype(jnp.bfloat16)
                    for j in range(ne):
                        x_ref[turn, j, :, pl.ds(start, sub)] = whole[j * chunk : (j + 1) * chunk]
                else:
                    cut_ref[0:modes, :] = real
                    cut_ref[modes:order, :] = imag
                    for j in range(ne):
                        x_ref[turn, j, :, pl.ds(start, sub)] = cut_ref[
                            pl.ds(j * chunk, chunk), :
                        ].astype(jnp.bfloat16)
                return carry

            lax.fori_loop(0, width // sub, body, 0)
            for d, other in enumerate(others + [chip]):
                slot = d * pieces + piece
                copy = remote(
                    part(x_ref.at[turn], other * 2 + 1 - core, piece),
                    part(pair.at[turn], d, piece),
                    sa.at[slot], ra.at[slot], "elec", partner,
                )
                copy.start()
                started.append(copy)
                first[d, piece] = copy

        def cross(piece):
            for d in range(chips - 1):
                slot = d * pieces + piece
                first[d, piece].wait_recv()
                half[turn, d, :, cut(piece)] = (
                    x_ref[turn, seats[d], :, cut(piece)].astype(jnp.float32)
                    + pair[turn, d, :, cut(piece)].astype(jnp.float32)
                ).astype(jnp.bfloat16)
                copy = remote(
                    part(half.at[turn], d, piece), part(far.at[turn], d, piece),
                    sb.at[slot], rb.at[slot], "elec", seats[d],
                )
                copy.start()
                started.append(copy)
                second[d, piece] = copy

        def close(piece):
            first[chips - 1, piece].wait_recv()
            total = x_ref[turn, me, :, cut(piece)].astype(jnp.float32) + pair[
                turn, chips - 1, :, cut(piece)
            ].astype(jnp.float32)
            for d in range(chips - 1):
                second[d, piece].wait_recv()
                total = total + far[turn, d, :, cut(piece)].astype(jnp.float32)
            gathered[me, :, cut(piece)] = total.astype(jnp.bfloat16)
            block = part(gathered, me, piece)
            for d in range(chips - 1):
                slot = d * pieces + piece
                copy = remote(block, block, sc.at[slot], rc.at[slot], "elec", seats[d])
                copy.start()
                started.append(copy)
            copy = remote(block, block, sd.at[piece], rd.at[piece], "elec", partner)
            copy.start()
            started.append(copy)

        def relay(piece):
            for d in range(chips - 1):
                slot = d * pieces + piece
                source = sources[d] * 2 + core
                block = part(gathered, source, piece)
                remote(block, block, sc.at[slot], rc.at[slot], "elec", source).wait_recv()
                copy = remote(block, block, se.at[slot], re.at[slot], "elec", partner)
                copy.start()
                started.append(copy)

        def arrive(piece):
            block = part(gathered, partner, piece)
            remote(block, block, sd.at[piece], rd.at[piece], "elec", partner).wait_recv()
            for d in range(chips - 1):
                slot = d * pieces + piece
                block = part(gathered, sources[d] * 2 + 1 - core, piece)
                remote(block, block, se.at[slot], re.at[slot], "elec", partner).wait_recv()
            finish(piece)

        for tick in range(pieces + 5):
            for lag, stage in ((0, compute), (1, cross), (3, close), (4, relay), (5, arrive)):
                if 0 <= tick - lag < pieces:
                    stage(tick - lag)
            if tick == pieces:
                beside()

    def stacked(gathered, start):
        if chunk % 16 == 0:
            return jnp.concatenate([gathered[j, :, pl.ds(start, sub)] for j in range(ne)], axis=0)
        for j in range(ne):
            cut_ref[pl.ds(j * chunk, chunk), :] = gathered[j, :, pl.ds(start, sub)].astype(
                jnp.float32
            )
        return cut_ref[...].astype(jnp.bfloat16)

    wide = rows_a.shape[1]
    split_rows(rows_a[:, 0:electrons])
    rows_a[...] = jnp.zeros_like(rows_a)

    def project_piece(piece):
        def body(step, carry):
            start = pl.multiple_of(piece * width + step * sub, 128)
            fields = stacked(first_ref, start)
            swapped = jnp.concatenate([-fields[modes:], fields[:modes]], axis=0)
            rows_a[:, 0:electrons] += dot(fields, waves_ref[:, pl.ds(start, sub)], NT) + dot(
                swapped, waves_ref[:, pl.ds(pl.multiple_of(pixels + start, 128), sub)], NT
            )
            rows_a[:, electrons : electrons + order] += dot(fields, fields, NT)
            return carry

        lax.fori_loop(0, width // sub, body, 0)

    round_trip(0, first_ref, project_piece, lambda: None)
    for j in range(np_):
        pay_ref[j] = rows_a[pl.ds(j * depth, depth), :]
    started += scatter_gather(
        np_, peers, pay_ref, held_b, total_b, ps.at[4], ps.at[5], ps.at[6], ps.at[7]
    )
    for j in range(np_):
        rows_a[pl.ds(j * depth, depth), :] = total_b[j]

    row_id = lax.broadcasted_iota(jnp.int32, (order, order), 0)
    col_id = lax.broadcasted_iota(jnp.int32, (order, order), 1)
    raw = rows_a[:, electrons : electrons + order]
    trace = 2.0 * jnp.sum(
        jnp.sum(jnp.where(row_id == col_id, raw, 0.0), axis=1, keepdims=True), axis=0, keepdims=True
    )
    split_rows(rows_a[:, 0:electrons] / jnp.sqrt(trace))

    def first_turn():
        gram_re = raw[:modes, :modes] + raw[modes:, modes:]
        gram_im = raw[:modes, modes:] - raw[modes:, :modes]
        emb_ref[0:modes, 0:modes] = gram_re
        emb_ref[0:modes, modes:order] = -gram_im
        emb_ref[modes:order, 0:modes] = gram_im
        emb_ref[modes:order, modes:order] = gram_re
        identity = jnp.where(row_id == col_id, 1.0, 0.0).astype(jnp.float32)
        turn_ref[...] = newton_schulz(emb_ref[...] / trace, identity)

    emb2 = [jnp.zeros((order, order), jnp.float32)]

    def gram_piece(piece):
        def body(step, carry):
            fields = stacked(applied_ref, pl.multiple_of(piece * width + step * sub, 128))
            return carry + dot(fields, fields, NT)

        emb2[0] = lax.fori_loop(0, width // sub, body, emb2[0])

    round_trip(1, applied_ref, gram_piece, first_turn)
    raw2 = emb2[0]
    gram_re = raw2[:modes, :modes] + raw2[modes:, modes:]
    gram_im = raw2[:modes, modes:] - raw2[modes:, :modes]
    low = modes // 2
    emb_ref[0:modes, 0:modes] = gram_re
    emb_ref[0:modes, modes:order] = gram_im
    gram_in[0, :, 0:order] = emb_ref[0:low, 0:order]
    gram_in[0, :, order : 2 * order] = emb_ref[low:modes, 0:order]
    last = []
    for d in range(1, np_):
        copy = remote(
            gram_in.at[0], gram_in.at[d], gs.at[0, d], gs.at[1, d], "pix", peers[d - 1]
        )
        copy.start()
        last.append(copy)
    total = gram_in[0]
    for d in range(1, np_):
        last[d - 1].wait_recv()
        total = total + gram_in[d]
    gram_ref[...] = total
    for copy in started + last:
        copy.wait_send()


def middle(waves, part, mode_count):
    np_ = lax.axis_size("pix")
    ne = lax.axis_size("elec")
    electrons = waves.shape[0]
    pixels = waves.shape[1] // 2
    order = 2 * mode_count
    chunk = order // ne
    depth = order // np_
    pieces = next(count for count in (4, 2, 1) if pixels % (128 * count) == 0)
    sub = next(size for size in (512, 640, 256, 128) if pixels // pieces % size == 0)
    chips = ne // 2
    wide = electrons + order + -order % 128
    vmem = pl.BlockSpec(memory_space=pltpu.VMEM)
    dma = pltpu.SemaphoreType.DMA
    f32, bf16 = jnp.float32, jnp.bfloat16
    return pl.pallas_call(
        functools.partial(core_kernel, np_, ne, pieces, sub, electrons, mode_count),
        out_shape=[
            jax.ShapeDtypeStruct((ne, chunk, pixels), bf16),
            jax.ShapeDtypeStruct((mode_count // 2, 2 * order), f32),
            jax.ShapeDtypeStruct((order, order), f32),
        ],
        in_specs=[vmem, vmem],
        out_specs=[vmem] * 3,
        scratch_shapes=[
            pltpu.VMEM((order, wide), f32),
            pltpu.VMEM((2 * order, electrons), bf16),
            pltpu.VMEM((order, sub), f32),
            pltpu.VMEM((order, order), f32),
            pltpu.VMEM((np_, depth, electrons), f32),
            pltpu.VMEM((np_, depth, electrons), f32),
            pltpu.VMEM((np_, depth, wide), f32),
            pltpu.VMEM((np_, depth, wide), f32),
            pltpu.VMEM((np_, depth, wide), f32),
            pltpu.VMEM((2, ne, chunk, pixels), bf16),
            pltpu.VMEM((2, chips, chunk, pixels), bf16),
            pltpu.VMEM((2, chips, chunk, pixels), bf16),
            pltpu.VMEM((2, chips, chunk, pixels), bf16),
            pltpu.VMEM((ne, chunk, pixels), bf16),
            pltpu.VMEM((np_, mode_count // 2, 2 * order), f32),
            dma((8, np_)),
            dma((20, chips * pieces)),
            dma((2, np_)),
        ],
        compiler_params=pltpu.CompilerParams(
            collective_id=1, has_side_effects=True, vmem_limit_bytes=60 * 1024 * 1024
        ),
        name="middle",
    )(waves, part.reshape(np_, depth, electrons))


def swap_kernel(n, axis, x_ref, out_ref, own_sem, send, recv):
    me = lax.axis_index(axis)
    peers = [lax.rem(me + d, n) for d in range(1, n)]
    greet((axis, peers))
    copies = []
    for d in range(1, n):
        copy = remote(
            x_ref.at[peers[d - 1]], out_ref.at[me], send.at[d], recv.at[d], axis, peers[d - 1]
        )
        copy.start()
        copies.append(copy)
    own = pltpu.make_async_copy(x_ref.at[me], out_ref.at[me], own_sem)
    own.start()
    own.wait()
    for d in range(1, n):
        source = lax.rem(me + n - d, n)
        remote(
            x_ref.at[source], out_ref.at[source], send.at[d], recv.at[d], axis, source
        ).wait_recv()
    for copy in copies:
        copy.wait_send()


def swap(value, axis, collective_id):
    n = lax.axis_size(axis)
    vmem = pl.BlockSpec(memory_space=pltpu.VMEM)
    dma = pltpu.SemaphoreType.DMA
    return pl.pallas_call(
        functools.partial(swap_kernel, n, axis),
        out_shape=jax.ShapeDtypeStruct(value.shape, value.dtype),
        in_specs=[vmem],
        out_specs=vmem,
        scratch_shapes=[dma, dma((n,)), dma((n,))],
        compiler_params=pltpu.CompilerParams(collective_id=collective_id, has_side_effects=True),
        name=f"swap_{axis}",
    )(value)


def project(wave_re, wave_im, stacked):
    half = stacked.shape[0] // 2
    swapped = jnp.concatenate([-stacked[half:], stacked[:half]], axis=0)
    contract = (((1,), (1,)), ((), ()))
    real_side = lax.dot_general(stacked, wave_re, contract, preferred_element_type=jnp.float32)
    imag_side = lax.dot_general(swapped, wave_im, contract, preferred_element_type=jnp.float32)
    return real_side + imag_side


def embed(gram_raw, mode_count):
    gram_re = gram_raw[:mode_count, :mode_count] + gram_raw[mode_count:, mode_count:]
    gram_im = gram_raw[:mode_count, mode_count:] - gram_raw[mode_count:, :mode_count]
    return jnp.concatenate(
        [jnp.concatenate([gram_re, -gram_im], 1), jnp.concatenate([gram_im, gram_re], 1)], 0
    )


def newton_schulz(scaled, identity):
    inverse_root = identity
    for step in range(NS_STEPS):
        product = scaled if step == 0 else jnp.dot(inverse_root, scaled, precision=HIGH)
        correction = 1.5 * identity - 0.5 * product
        if step == 0:
            inverse_root = correction
        else:
            inverse_root = jnp.dot(correction, inverse_root, precision=HIGH)
        if step + 1 < NS_STEPS:
            scaled = jnp.dot(scaled, correction, precision=HIGH)
    return inverse_root


def dft_table(length):
    index = np.arange(length, dtype=np.int64)
    angle = 2.0 * np.pi / length * (index[:, None] * index[None, :] % length)
    return np.cos(angle).astype(np.float32), -np.sin(angle).astype(np.float32)


def split(table):
    upper = table.astype(jnp.bfloat16)
    lower = (table - upper.astype(np.float32)).astype(jnp.bfloat16)
    return upper, lower


def chirp_phase(row_pos, col_pos, row_total, col_total, factor):
    row_term = (row_pos - row_total / 2.0) ** 2 / row_total
    col_term = (col_pos - col_total / 2.0) ** 2 / col_total
    angle = math.pi * factor * (row_term[:, None] + col_term[None, :])
    return (jnp.cos(angle), jnp.sin(angle))


def column_section(field, row_pos, row_total, col_total, pix_count):
    share, rows_dev = field.shape[1], field.shape[2]
    col_pos = jnp.arange(col_total, dtype=jnp.float32)
    chirp_re, chirp_im = chirp_phase(row_pos, col_pos, row_total, col_total, 0.5)
    launch_re = chirp_re * field[0] - chirp_im * field[1]
    launch_im = chirp_re * field[1] + chirp_im * field[0]
    table_re, table_im = dft_table(col_total)
    both = np.concatenate([table_re, table_im], axis=1)
    launch = jnp.stack([launch_re, launch_im]).reshape(2 * share * rows_dev, col_total)
    wide = jnp.dot(launch, jnp.asarray(both), precision=lax.Precision.HIGH)
    wide = wide.reshape(2, share, rows_dev, 2, pix_count, col_total // pix_count)
    spec_re = wide[0, :, :, 0] - wide[1, :, :, 1]
    spec_im = wide[0, :, :, 1] + wide[1, :, :, 0]
    spec = jnp.stack([spec_re, spec_im]).astype(jnp.bfloat16)
    return spec.transpose(3, 2, 0, 1, 4).reshape(pix_count, rows_dev, -1)


def row_section(spectrum, share, col_pos, row_total, col_total):
    width = col_pos.shape[0]
    table_re, table_im = dft_table(row_total)
    upper, lower = split(np.concatenate([table_re, table_im], axis=0))
    tables = np.concatenate([upper, lower], axis=0)
    wide = jnp.dot(jnp.asarray(tables), spectrum, preferred_element_type=jnp.float32)
    wide = wide[: 2 * row_total] + wide[2 * row_total :]
    half = share * width
    out_re = wide[:row_total, :half] - wide[row_total:, half:]
    out_im = wide[:row_total, half:] + wide[row_total:, :half]
    row_pos = jnp.arange(row_total, dtype=jnp.float32)
    chirp_re, chirp_im = chirp_phase(row_pos, col_pos, row_total, col_total, 0.25)
    out_re = out_re.reshape(row_total, share, width).transpose(1, 0, 2)
    out_im = out_im.reshape(row_total, share, width).transpose(1, 0, 2)
    return jnp.stack([chirp_re * out_re - chirp_im * out_im, chirp_re * out_im + chirp_im * out_re])


def shards(wavefronts, trial_modes):
    electrons_dev, _, rows_dev, cols = wavefronts.shape
    mode_count = trial_modes.shape[1]
    order = 2 * mode_count
    pixels = rows_dev * cols
    groups = lax.axis_size("elec")
    share = mode_count // groups
    waves = wavefronts.reshape(electrons_dev, 2 * pixels)
    low = trial_modes.astype(jnp.bfloat16).reshape(order, pixels)

    part = project(waves[:, :pixels], waves[:, pixels:], low)
    applied, packed, inverse_root = middle(waves, part, mode_count)
    applied = applied.reshape(order, pixels)
    turn = inverse_root.T
    gram = jnp.concatenate([packed[:, :order], packed[:, order:]], axis=0)
    gram_re, gram_im = gram[:, :mode_count], gram[:, mode_count:]
    raw = jnp.concatenate(
        [jnp.concatenate([gram_re, gram_im], 1), jnp.concatenate([-gram_im, gram_re], 1)], 0
    )
    raw = 0.5 * jnp.dot(jnp.dot(turn, raw, precision=HIGH), inverse_root, precision=HIGH)
    embedded = embed(raw, mode_count)
    trace_value = jnp.trace(embedded)
    identity = jnp.eye(order, dtype=jnp.float32)
    last = (newton_schulz(embedded / trace_value, identity) / jnp.sqrt(trace_value)).T
    turn = jnp.dot(last, turn, precision=HIGH)
    mine = lax.dynamic_slice_in_dim(
        turn.reshape(2, mode_count, 2 * mode_count), lax.axis_index("elec") * share, share, axis=1
    ).reshape(2 * share, 2 * mode_count)
    mine_upper = lax.reduce_precision(mine, 8, 7)
    mine_lower = (mine - mine_upper).astype(jnp.bfloat16)
    field = jnp.dot(
        mine_upper.astype(jnp.bfloat16), applied, preferred_element_type=jnp.float32
    ) + jnp.dot(mine_lower, applied, preferred_element_type=jnp.float32)
    field = field.reshape(2, share, rows_dev, cols)

    pix_count = lax.axis_size("pix")
    row_total = rows_dev * pix_count
    row_pos = (lax.axis_index("pix") * rows_dev + jnp.arange(rows_dev, dtype=jnp.int32)).astype(
        jnp.float32
    )
    spectrum = column_section(field, row_pos, row_total, cols, pix_count)
    column_block = swap(spectrum, "pix", 2).reshape(row_total, -1)
    width = cols // pix_count
    col_pos = (lax.axis_index("pix") * width + jnp.arange(width, dtype=jnp.int32)).astype(
        jnp.float32
    )
    return row_section(column_block, share, col_pos, row_total, cols)


def solution(mesh):
    in_specs = (P("elec", None, "pix", None), P(None, None, "pix", None))
    out_specs = P(None, "elec", None, "pix")
    return jax.shard_map(shards, mesh=mesh, in_specs=in_specs, out_specs=out_specs, check_vma=False)
```

time: 180 us -> 140 us (0.78)
  matrix products: 51.4 us -> 17.8 us
  other arithmetic: 12.1 us -> 5.6 us
    dot_general x7 -> x3, matrix products: 18.5 us -> 2.17 us  [the longest x1 1.02 us: shards(): jnp.dot(turn, raw, precision=HIGH)]
    dot_general x2 -> x1, matrix products: 8.38 us -> 2.51 us  [project(): lax.dot_general(swapped, wave_im, contract, preferred_element_type=jnp.fl...]
    dot_general x2 -> x1, matrix products: 9 us -> 3.2 us  [project(): lax.dot_general(stacked, wave_re, contract, preferred_element_type=jnp.fl...]
    pallas_call x1, Pallas kernels: 8.66 us -> 11.2 us  [swap(): pl.pallas_call(functools.partial(swap_kernel, n, axis), out_shape=jax.Sha...]
    concatenate x2 -> x0, other arithmetic: 2.31 us -> none  [covariance(): return jnp.concatenate([real_part, imag_part], axis=0)]
    dot_general x14 -> x7, matrix products: 3.72 us -> 1.86 us  [newton_schulz(): jnp.dot(inverse_root, scaled, precision=HIGH)]
    dot_general x14 -> x7, matrix products: 3.71 us -> 1.85 us  [newton_schulz(): inverse_root = jnp.dot(correction, inverse_root, precision=HIGH)]
    dot_general x14 -> x7, matrix products: 3.81 us -> 1.95 us  [newton_schulz(): scaled = jnp.dot(scaled, correction, precision=HIGH)]
where the time goes in v2:
time: 140 us
  Pallas kernels  95.3 us (68%)
  local copies, waits for them, and re-layouts  19.6 us (14%)
  matrix products  17.8 us (13%)
  other arithmetic  5.6 us (4%)
    pallas_call x1, Pallas kernels, middle(): pl.pallas_call(functools.partial(core_kernel, np_, ne, pieces, sub, elect...  84.1 us
    unnamed x14, local copies, waits for them, and re-layouts  15.2 us
    pallas_call x1, Pallas kernels, swap(): pl.pallas_call(functools.partial(swap_kernel, n, axis), out_shape=jax.Sha...  11.2 us
    dot_general x1, matrix products, project(): lax.dot_general(stacked, wave_re, contract, preferred_element_type=jnp.fl...  3.2 us

profile of v2, /device:TPU:0, one launch (start us, length us, event | category | flops | bytes accessed | tf_op | source)
XLA Modules:
  0.0 139.5 jit_solution(15174285848887509438)
XLA Ops:
  0.5 1.9 %convert_element_type.33 = bf16[2,32,40,256]{3,2,1,0:T(8,128)(2,1)S(1)} convert(f32[2,32,40,256]{3,2,1,0:T(8,128)} %param.5) | non-fusion elementwise | flops 655360 | bytes 3932160 | tf_op jit(solution)/shard_map/convert_element_type | solution.py:482
  2.4 0.3 copy.30
  3.0 11.0 %copy.29 = bf16[48,8,80,256]{3,1,2,0:T(8,128)(2,1)S(1)} copy(bf16[48,8,80,256]{3,2,1,0:T(8,128)(2,1)} %bitcast.117) | data formatting | bytes 31457280
  14.0 2.5 %fusion = f32[64,384]{1,0:T(8,128)S(1)} fusion(bf16[384,20480]{1,0:T(8,128)(2,1)S(1)} %bitcast.114, bf16[32,10240]{1,0:T(8,128)(2,1)S(1)} %bitcast.130, bf16[32,10240]{1,0:T(8,128)(2,1)S(1)} %bitcast.129), kind=kOutput, calls=%fused_computation.1 | convolution fusion | flops 505937920 | bytes 9273344 | tf_op jit(solution)/shard_map/dot_general | solution.py:395
  16.5 3.0 %copy-done = bf16[48,8,80,256]{3,1,2,0:T(8,128)(2,1)} copy-done((bf16[48,8,80,256]{3,1,2,0:T(8,128)(2,1)}, bf16[48,8,80,256]{3,1,2,0:T(8,128)(2,1)S(1)}, u32[]{:S(2)}) %copy-start) | copy-done | bytes 15728664
  19.5 3.2 %fusion.10.part_ref = f32[8,8,384]{2,1,0:T(8,128)} fusion(f32[64,384]{1,0:T(8,128)S(1)} %fusion, bf16[64,10240]{1,0:T(8,128)(2,1)S(1)} %bitcast.125, bf16[384,20480]{1,0:T(8,128)(2,1)S(1)} %bitcast.115), kind=kOutput, calls=%fused_computation.10 | convolution fusion | flops 503341056 | bytes 9371648 | tf_op jit(solution)/shard_map/dot_general | solution.py:394
  22.7 84.1 %middle.1 = (bf16[4,16,10240]{2,1,0:T(8,128)(2,1)}, f32[16,128]{1,0:T(8,128)}, f32[64,64]{1,0:T(8,128)}) custom-call(bf16[384,20480]{1,0:T(8,128)(2,1)} %bitcast.116, f32[8,8,384]{2,1,0:T(8,128)} %fusion.10.part_ref), custom_call_target="tpu_custom_call" | custom-call | tf_op jit(solution)/shard_map/middle/pallas_call | solution.py:316
  106.8 0.8 fusion.74
  107.7 1.0 fusion.34
  108.7 0.9 convolution_multiply_fusion.7
  109.7 0.7 select_reduce_fusion
  111.1 1.0 fusion.42
  112.1 0.9 fusion.19
  113.0 0.9 fusion.41
  117.2 0.3 fusion.56
  117.5 0.3 convolution_add_fusion
  118.1 0.8 copy-done.3
  118.9 1.9 %fusion.23 = f32[2,8,40,2,8,32]{2,5,4,3,1,0:T(8,128)S(1)} fusion(f32[2,8,32,256,1,1]{3,2,1,0,5,4:T(8,128)S(1)} %copy-done.3, f32[1,8,40,256]{3,2,1,0:T(8,128)S(1)} %get-tuple-element.20, f32[1,8,40,256]{3,2,1,0:T(8,128)S(1)} %get-tuple-element.19), kind=kOutput, calls=%fused_computation.37 | convolution fusion | flops 503480320 | bytes 2490368 | tf_op jit(solution)/shard_map/dot_general | solution.py:449
  121.5 1.2 copy.22
  122.7 2.0 %reshape.272.x_ref = bf16[8,40,512]{2,1,0:T(8,128)(2,1)} reshape(bf16[8,40,2,8,32]{4,3,2,1,0:T(8,128)(2,1)S(1)} %copy.22) | data formatting | bytes 655360 | tf_op jit(solution)/shard_map/reshape | solution.py:454
  124.7 11.2 %swap_pix.1 = bf16[8,40,512]{2,1,0:T(8,128)(2,1)} custom-call(bf16[8,40,512]{2,1,0:T(8,128)(2,1)} %reshape.272.x_ref), custom_call_target="tpu_custom_call" | custom-call | tf_op jit(solution)/shard_map/swap_pix/pallas_call | solution.py:379
  135.9 1.8 %fusion.87 = f32[1280,512]{1,0:T(8,128)S(1)} fusion(bf16[1280,320]{1,0:T(8,128)(2,1)S(1)} %copy-done.2, bf16[320,512]{1,0:T(8,128)(2,1)} %bitcast.128), kind=kOutput, calls=%fused_computation.121 | convolution fusion | flops 419430400 | bytes 3768320 | tf_op jit(solution)/shard_map/dot_general | solution.py:462
  137.7 0.3 slice_add_fusion
  138.6 0.9 pad_maximum_fusion
  (47 shorter events, 5.6 us)
Async XLA Ops:
  14.0 5.5 %copy-start = (bf16[48,8,80,256]{3,1,2,0:T(8,128)(2,1)}, bf16[48,8,80,256]{3,1,2,0:T(8,128)(2,1)S(1)}, u32[]{:S(2)}) copy-start(bf16[48,8,80,256]{3,1,2,0:T(8,128)(2,1)S(1)} %copy.29) | copy-start | bytes 47185924
  109.7 7.2 %copy-start.4 = (f32[64,64]{1,0:T(8,128)S(1)}, f32[64,64]{1,0:T(8,128)}, u32[]{:S(2)}) copy-start(f32[64,64]{1,0:T(8,128)} %get-tuple-element.8) | copy-start | bytes 49156
  111.1 6.1 %copy-start.1 = (bf16[4,16,10240]{2,1,0:T(8,128)(2,1)S(1)}, bf16[4,16,10240]{2,1,0:T(8,128)(2,1)}, u32[]{:S(2)}) copy-start(bf16[4,16,10240]{2,1,0:T(8,128)(2,1)} %get-tuple-element.10) | copy-start | bytes 3932164
  117.8 1.0 copy-start.3
  122.7 13.2 %copy-start.2 = (bf16[1280,320]{1,0:T(8,128)(2,1)S(1)}, bf16[1280,320]{1,0:T(8,128)(2,1)}, u32[]{:S(2)}) copy-start(bf16[1280,320]{1,0:T(8,128)(2,1)} %constant.55.clone) | copy-start | bytes 2457604

commit v3 on v2

--- a/solution.py
+++ b/solution.py
@@ -71,13 +71,15 @@
 
 def core_kernel(
     np_, ne, pieces, sub, electrons, modes,
-    waves_ref, part_ref,
-    applied_ref, gram_ref, turn_ref,
-    rows_a, both_ref, cut_ref, emb_ref,
+    waves_ref, low_ref, chirp_ref, table_ref,
+    out_ref,
+    applied_ref, turn_ref, part_ref, lines_ref, launch_ref, spec_ref, send_ref, rows_a, both_ref, cut_ref, emb_ref,
     held_a, total_a, pay_ref, held_b, total_b,
     x_ref, pair, half, far, first_ref, gram_in,
     ps, es, gs,
 ):
+    share = modes // ne
+    rows, cols = chirp_ref.shape[1], chirp_ref.shape[2]
     pixels = waves_ref.shape[1] // 2
     order = 2 * modes
     chunk = order // ne
@@ -93,6 +95,22 @@
     others = [lax.rem(chip + d, chips) for d in range(1, chips)]
     seats = [other * 2 + core for other in others]
     sources = [lax.rem(chip + chips - d, chips) for d in range(1, chips)]
+    rows_a[...] = jnp.zeros_like(rows_a)
+
+    def correlate(fields, start):
+        swapped = jnp.concatenate([-fields[modes:], fields[:modes]], axis=0)
+        rows_a[:, 0:electrons] += dot(fields, waves_ref[:, pl.ds(start, sub)], NT) + dot(
+            swapped, waves_ref[:, pl.ds(pl.multiple_of(pixels + start, 128), sub)], NT
+        )
+
+    def opening(step, carry):
+        start = pl.multiple_of(step * sub, 128)
+        correlate(low_ref[:, pl.ds(start, sub)], start)
+        return carry
+
+    lax.fori_loop(0, pixels // sub, opening, 0)
+    for j in range(np_):
+        part_ref[j] = rows_a[pl.ds(j * depth, depth), 0:electrons]
     greet(("pix", peers), ("elec", [partner] + seats))
     started = scatter_gather(
         np_, peers, part_ref, held_a, total_a, ps.at[0], ps.at[1], ps.at[2], ps.at[3]
@@ -220,7 +238,6 @@
             )
         return cut_ref[...].astype(jnp.bfloat16)
 
-    wide = rows_a.shape[1]
     split_rows(rows_a[:, 0:electrons])
     rows_a[...] = jnp.zeros_like(rows_a)
 
@@ -228,10 +245,7 @@
         def body(step, carry):
             start = pl.multiple_of(piece * width + step * sub, 128)
             fields = stacked(first_ref, start)
-            swapped = jnp.concatenate([-fields[modes:], fields[:modes]], axis=0)
-            rows_a[:, 0:electrons] += dot(fields, waves_ref[:, pl.ds(start, sub)], NT) + dot(
-                swapped, waves_ref[:, pl.ds(pl.multiple_of(pixels + start, 128), sub)], NT
-            )
+            correlate(fields, start)
             rows_a[:, electrons : electrons + order] += dot(fields, fields, NT)
             return carry
 
@@ -293,12 +307,111 @@
     for d in range(1, np_):
         last[d - 1].wait_recv()
         total = total + gram_in[d]
-    gram_ref[...] = total
-    for copy in started + last:
+    emb_ref[0:low, 0:order] = total[:, 0:order]
+    emb_ref[low:modes, 0:order] = total[:, order : 2 * order]
+    gram_re = emb_ref[0:modes, 0:modes]
+    gram_im = emb_ref[0:modes, modes:order]
+    emb_ref[0:modes, modes:order] = gram_im
+    emb_ref[modes:order, 0:modes] = -gram_im
+    emb_ref[modes:order, modes:order] = gram_re
+    first_root = turn_ref[...]
+    first_t = first_root.T
+    raw = 0.5 * jnp.dot(
+        jnp.dot(first_t, emb_ref[...], precision=HIGH), first_root, precision=HIGH
+    )
+    gram_re = raw[:modes, :modes] + raw[modes:, modes:]
+    gram_im = raw[:modes, modes:] - raw[modes:, :modes]
+    emb_ref[0:modes, 0:modes] = gram_re
+    emb_ref[0:modes, modes:order] = -gram_im
+    emb_ref[modes:order, 0:modes] = gram_im
+    emb_ref[modes:order, modes:order] = gram_re
+    embedded = emb_ref[...]
+    diagonal = row_id == col_id
+    trace = jnp.sum(
+        jnp.sum(jnp.where(diagonal, embedded, 0.0), axis=1, keepdims=True), axis=0, keepdims=True
+    )
+    identity = jnp.where(diagonal, 1.0, 0.0).astype(jnp.float32)
+    second_root = newton_schulz(embedded / trace, identity) / jnp.sqrt(trace)
+    turn_ref[...] = jnp.dot(second_root.T, first_t, precision=HIGH)
+    for part_of in range(2):
+        emb_ref[pl.ds(part_of * share, share), :] = turn_ref[
+            pl.ds(part_of * modes + me * share, share), :
+        ]
+    mine = emb_ref[0 : 2 * share, :]
+    upper = mine.astype(jnp.bfloat16)
+    lower = (mine - upper.astype(jnp.float32)).astype(jnp.bfloat16)
+    group = next(count for count in (8, 5, 4, 2, 1) if rows % count == 0)
+
+    def rotate(step, carry):
+        start = pl.multiple_of(step * (group * cols), 128)
+        if chunk % 16 == 0:
+            fields = jnp.concatenate(
+                [applied_ref[j, :, pl.ds(start, group * cols)] for j in range(ne)], axis=0
+            )
+        else:
+            fields = jnp.concatenate(
+                [
+                    applied_ref[j, :, pl.ds(start, group * cols)].astype(jnp.float32)
+                    for j in range(ne)
+                ],
+                axis=0,
+            ).astype(jnp.bfloat16)
+        turned = dot(upper, fields, NN) + dot(lower, fields, NN)
+        for i in range(group):
+            for b in range(cols // 128):
+                lines_ref[b, pl.ds((step * group + i) * 2 * share, 2 * share), :] = turned[
+                    :, i * cols + b * 128 : i * cols + (b + 1) * 128
+                ]
+        return carry
+
+    lax.fori_loop(0, rows // group, rotate, 0)
+    chirp_re, chirp_im = chirp_ref[0], chirp_ref[1]
+    for m in range(share):
+        real = jnp.concatenate(
+            [lines_ref[b, pl.ds(m, rows, stride=2 * share), :] for b in range(cols // 128)], axis=1
+        )
+        imag = jnp.concatenate(
+            [
+                lines_ref[b, pl.ds(share + m, rows, stride=2 * share), :]
+                for b in range(cols // 128)
+            ],
+            axis=1,
+        )
+        launch_ref[m * rows : (m + 1) * rows, 0:cols] = chirp_re * real - chirp_im * imag
+        launch_ref[m * rows : (m + 1) * rows, cols : 2 * cols] = chirp_re * imag + chirp_im * real
+    launch = launch_ref[...]
+    upper = launch.astype(jnp.bfloat16)
+    lower = (launch - upper.astype(jnp.float32)).astype(jnp.bfloat16)
+    spec_ref[...] = (
+        dot(upper, table_ref[0], NN) + dot(upper, table_ref[1], NN) + dot(lower, table_ref[0], NN)
+    )
+    thin = cols // np_
+    for p in range(np_):
+        for c in range(2):
+            for m in range(share):
+                at = (2 * p + c) * thin
+                to = (c * share + m) * thin
+                send_ref[p, :, to : to + thin] = spec_ref[
+                    m * rows : (m + 1) * rows, at : at + thin
+                ].astype(jnp.bfloat16)
+    swaps = []
+    for d in range(1, np_):
+        copy = remote(
+            send_ref.at[peers[d - 1]], out_ref.at[me_p], gs.at[2, d], gs.at[3, d], "pix",
+            peers[d - 1],
+        )
+        copy.start()
+        swaps.append(copy)
+    out_ref[me_p] = send_ref[me_p]
+    for d in range(1, np_):
+        source = lax.rem(me_p + np_ - d, np_)
+        block = out_ref.at[source]
+        remote(block, block, gs.at[2, d], gs.at[3, d], "pix", source).wait_recv()
+    for copy in started + last + swaps:
         copy.wait_send()
 
 
-def middle(waves, part, mode_count):
+def middle(waves, low, chirp, tables, mode_count):
     np_ = lax.axis_size("pix")
     ne = lax.axis_size("elec")
     electrons = waves.shape[0]
@@ -310,19 +423,25 @@
     sub = next(size for size in (512, 640, 256, 128) if pixels // pieces % size == 0)
     chips = ne // 2
     wide = electrons + order + -order % 128
+    share = mode_count // ne
+    rows, cols = chirp.shape[1:]
+    lanes = 2 * share * (cols // np_)
     vmem = pl.BlockSpec(memory_space=pltpu.VMEM)
     dma = pltpu.SemaphoreType.DMA
     f32, bf16 = jnp.float32, jnp.bfloat16
     return pl.pallas_call(
         functools.partial(core_kernel, np_, ne, pieces, sub, electrons, mode_count),
-        out_shape=[
-            jax.ShapeDtypeStruct((ne, chunk, pixels), bf16),
-            jax.ShapeDtypeStruct((mode_count // 2, 2 * order), f32),
-            jax.ShapeDtypeStruct((order, order), f32),
-        ],
-        in_specs=[vmem, vmem],
-        out_specs=[vmem] * 3,
+        out_shape=jax.ShapeDtypeStruct((np_, rows, lanes), bf16),
+        in_specs=[vmem] * 4,
+        out_specs=vmem,
         scratch_shapes=[
+            pltpu.VMEM((ne, chunk, pixels), bf16),
+            pltpu.VMEM((order, order), f32),
+            pltpu.VMEM((np_, depth, electrons), f32),
+            pltpu.VMEM((cols // 128, rows * 2 * share, 128), f32),
+            pltpu.VMEM((share * rows, 2 * cols), f32),
+            pltpu.VMEM((share * rows, 2 * cols), f32),
+            pltpu.VMEM((np_, rows, lanes), bf16),
             pltpu.VMEM((order, wide), f32),
             pltpu.VMEM((2 * order, electrons), bf16),
             pltpu.VMEM((order, sub), f32),
@@ -340,68 +459,13 @@
             pltpu.VMEM((np_, mode_count // 2, 2 * order), f32),
             dma((8, np_)),
             dma((20, chips * pieces)),
-            dma((2, np_)),
+            dma((4, np_)),
         ],
         compiler_params=pltpu.CompilerParams(
             collective_id=1, has_side_effects=True, vmem_limit_bytes=60 * 1024 * 1024
         ),
         name="middle",
-    )(waves, part.reshape(np_, depth, electrons))
-
-
-def swap_kernel(n, axis, x_ref, out_ref, own_sem, send, recv):
-    me = lax.axis_index(axis)
-    peers = [lax.rem(me + d, n) for d in range(1, n)]
-    greet((axis, peers))
-    copies = []
-    for d in range(1, n):
-        copy = remote(
-            x_ref.at[peers[d - 1]], out_ref.at[me], send.at[d], recv.at[d], axis, peers[d - 1]
-        )
-        copy.start()
-        copies.append(copy)
-    own = pltpu.make_async_copy(x_ref.at[me], out_ref.at[me], own_sem)
-    own.start()
-    own.wait()
-    for d in range(1, n):
-        source = lax.rem(me + n - d, n)
-        remote(
-            x_ref.at[source], out_ref.at[source], send.at[d], recv.at[d], axis, source
-        ).wait_recv()
-    for copy in copies:
-        copy.wait_send()
-
-
-def swap(value, axis, collective_id):
-    n = lax.axis_size(axis)
-    vmem = pl.BlockSpec(memory_space=pltpu.VMEM)
-    dma = pltpu.SemaphoreType.DMA
-    return pl.pallas_call(
-        functools.partial(swap_kernel, n, axis),
-        out_shape=jax.ShapeDtypeStruct(value.shape, value.dtype),
-        in_specs=[vmem],
-        out_specs=vmem,
-        scratch_shapes=[dma, dma((n,)), dma((n,))],
-        compiler_params=pltpu.CompilerParams(collective_id=collective_id, has_side_effects=True),
-        name=f"swap_{axis}",
-    )(value)
-
-
-def project(wave_re, wave_im, stacked):
-    half = stacked.shape[0] // 2
-    swapped = jnp.concatenate([-stacked[half:], stacked[:half]], axis=0)
-    contract = (((1,), (1,)), ((), ()))
-    real_side = lax.dot_general(stacked, wave_re, contract, preferred_element_type=jnp.float32)
-    imag_side = lax.dot_general(swapped, wave_im, contract, preferred_element_type=jnp.float32)
-    return real_side + imag_side
-
-
-def embed(gram_raw, mode_count):
-    gram_re = gram_raw[:mode_count, :mode_count] + gram_raw[mode_count:, mode_count:]
-    gram_im = gram_raw[:mode_count, mode_count:] - gram_raw[mode_count:, :mode_count]
-    return jnp.concatenate(
-        [jnp.concatenate([gram_re, -gram_im], 1), jnp.concatenate([gram_im, gram_re], 1)], 0
-    )
+    )(waves, low, chirp, tables)
 
 
 def newton_schulz(scaled, identity):
@@ -437,21 +501,11 @@
     return (jnp.cos(angle), jnp.sin(angle))
 
 
-def column_section(field, row_pos, row_total, col_total, pix_count):
-    share, rows_dev = field.shape[1], field.shape[2]
-    col_pos = jnp.arange(col_total, dtype=jnp.float32)
-    chirp_re, chirp_im = chirp_phase(row_pos, col_pos, row_total, col_total, 0.5)
-    launch_re = chirp_re * field[0] - chirp_im * field[1]
-    launch_im = chirp_re * field[1] + chirp_im * field[0]
-    table_re, table_im = dft_table(col_total)
-    both = np.concatenate([table_re, table_im], axis=1)
-    launch = jnp.stack([launch_re, launch_im]).reshape(2 * share * rows_dev, col_total)
-    wide = jnp.dot(launch, jnp.asarray(both), precision=lax.Precision.HIGH)
-    wide = wide.reshape(2, share, rows_dev, 2, pix_count, col_total // pix_count)
-    spec_re = wide[0, :, :, 0] - wide[1, :, :, 1]
-    spec_im = wide[0, :, :, 1] + wide[1, :, :, 0]
-    spec = jnp.stack([spec_re, spec_im]).astype(jnp.bfloat16)
-    return spec.transpose(3, 2, 0, 1, 4).reshape(pix_count, rows_dev, -1)
+def column_tables(length, pix_count):
+    table_re, table_im = dft_table(length)
+    full = np.stack([np.stack([table_re, table_im], 1), np.stack([-table_im, table_re], 1)])
+    full = full.reshape(2, length, 2, pix_count, length // pix_count).transpose(0, 1, 3, 2, 4)
+    return np.stack(split(full.reshape(2 * length, 2 * length)))
 
 
 def row_section(spectrum, share, col_pos, row_total, col_total):
@@ -481,38 +535,16 @@
     waves = wavefronts.reshape(electrons_dev, 2 * pixels)
     low = trial_modes.astype(jnp.bfloat16).reshape(order, pixels)
 
-    part = project(waves[:, :pixels], waves[:, pixels:], low)
-    applied, packed, inverse_root = middle(waves, part, mode_count)
-    applied = applied.reshape(order, pixels)
-    turn = inverse_root.T
-    gram = jnp.concatenate([packed[:, :order], packed[:, order:]], axis=0)
-    gram_re, gram_im = gram[:, :mode_count], gram[:, mode_count:]
-    raw = jnp.concatenate(
-        [jnp.concatenate([gram_re, gram_im], 1), jnp.concatenate([-gram_im, gram_re], 1)], 0
-    )
-    raw = 0.5 * jnp.dot(jnp.dot(turn, raw, precision=HIGH), inverse_root, precision=HIGH)
-    embedded = embed(raw, mode_count)
-    trace_value = jnp.trace(embedded)
-    identity = jnp.eye(order, dtype=jnp.float32)
-    last = (newton_schulz(embedded / trace_value, identity) / jnp.sqrt(trace_value)).T
-    turn = jnp.dot(last, turn, precision=HIGH)
-    mine = lax.dynamic_slice_in_dim(
-        turn.reshape(2, mode_count, 2 * mode_count), lax.axis_index("elec") * share, share, axis=1
-    ).reshape(2 * share, 2 * mode_count)
-    mine_upper = lax.reduce_precision(mine, 8, 7)
-    mine_lower = (mine - mine_upper).astype(jnp.bfloat16)
-    field = jnp.dot(
-        mine_upper.astype(jnp.bfloat16), applied, preferred_element_type=jnp.float32
-    ) + jnp.dot(mine_lower, applied, preferred_element_type=jnp.float32)
-    field = field.reshape(2, share, rows_dev, cols)
-
     pix_count = lax.axis_size("pix")
     row_total = rows_dev * pix_count
     row_pos = (lax.axis_index("pix") * rows_dev + jnp.arange(rows_dev, dtype=jnp.int32)).astype(
         jnp.float32
     )
-    spectrum = column_section(field, row_pos, row_total, cols, pix_count)
-    column_block = swap(spectrum, "pix", 2).reshape(row_total, -1)
+    chirp = jnp.stack(
+        chirp_phase(row_pos, jnp.arange(cols, dtype=jnp.float32), row_total, cols, 0.5)
+    )
+    tables = jnp.asarray(column_tables(cols, pix_count))
+    column_block = middle(waves, low, chirp, tables, mode_count).reshape(row_total, -1)
     width = cols // pix_count
     col_pos = (lax.axis_index("pix") * width + jnp.arange(width, dtype=jnp.int32)).astype(
         jnp.float32

time: 140 us -> 129 us (0.921)
  matrix products: 17.8 us -> 1.81 us
  Pallas kernels: 95.3 us -> 106 us
  local copies, waits for them, and re-layouts: 19.6 us -> 16.9 us
    pallas_call x1, Pallas kernels: 84.1 us -> 106 us  [middle(): pl.pallas_call(functools.partial(core_kernel, np_, ne, pieces, sub, elect...]
    dot_general x29 -> x0, matrix products: 16 us -> none  [the longest x1 3.2 us: project(): lax.dot_general(stacked, wave_re, contract, preferred_element_type=jnp.fl...]
    pallas_call x1 -> x0, Pallas kernels: 11.2 us -> none  [swap(): pl.pallas_call(functools.partial(swap_kernel, n, axis), out_shape=jax.Sha...]
    reshape x1 -> x0, local copies, waits for them, and re-layouts: 2.01 us -> none  [column_section(): return spec.transpose(3, 2, 0, 1, 4).reshape(pix_count, rows_dev, -1)]
    unnamed x14 -> x4, local copies, waits for them, and re-layouts: 15.2 us -> 16.6 us
where the time goes in v3:
time: 129 us
  Pallas kernels  106 us (82%)
  local copies, waits for them, and re-layouts  16.9 us (13%)
  other arithmetic  4.43 us (3%)
  matrix products  1.81 us (1%)
    pallas_call x1, Pallas kernels, middle(): pl.pallas_call(functools.partial(core_kernel, np_, ne, pieces, sub, elect...  106 us
    unnamed x4, local copies, waits for them, and re-layouts  16.6 us

profile of v3, /device:TPU:0, one launch (start us, length us, event | category | flops | bytes accessed | tf_op | source)
XLA Modules:
  0.0 128.9 jit_solution(13424942520094197002)
XLA Ops:
  0.0 0.2 fusion.3
  0.3 0.6 pad_maximum_fusion.1.chirp_ref
  0.9 0.3 fusion.1
  1.2 1.9 %convert_element_type.18 = bf16[2,32,40,256]{3,2,1,0:T(8,128)(2,1)S(1)} convert(f32[2,32,40,256]{3,2,1,0:T(8,128)} %param.5) | non-fusion elementwise | flops 655360 | bytes 3932160 | tf_op jit(solution)/shard_map/convert_element_type | solution.py:536
  3.0 1.3 %copy.12 = bf16[8,8,40,256]{3,1,2,0:T(8,128)(2,1)} copy(bf16[8,8,40,256]{3,2,1,0:T(8,128)(2,1)S(1)} %bitcast.21) | data formatting | bytes 2621440
  4.4 15.2 %copy.11 = bf16[48,8,80,256]{3,1,2,0:T(8,128)(2,1)} copy(bf16[48,8,80,256]{3,2,1,0:T(8,128)(2,1)} %bitcast.20) | data formatting | bytes 31457280
  19.6 0.0 copy-start
  19.6 105.7 %middle.1 = bf16[8,40,512]{2,1,0:T(8,128)(2,1)} custom-call(bf16[384,20480]{1,0:T(8,128)(2,1)} %bitcast.19, bf16[64,10240]{1,0:T(8,128)(2,1)} %bitcast.22, f32[2,40,256]{2,1,0:T(8,128)} %pad_maximum_fusion.1.chirp_ref, bf16[2,512,512]{2,1,0:T(8,128)(2,1)} %constant.36.clone.table_ref), custom_call_target="tpu_custom_call" | custom-call | tf_op jit(solution)/shard_map/middle/pallas_call | solution.py:432
  125.3 0.0 copy-done
  125.3 1.8 %fusion.4 = f32[1280,512]{1,0:T(8,128)S(1)} fusion(bf16[1280,320]{1,0:T(8,128)(2,1)S(1)} %copy-done, bf16[320,512]{1,0:T(8,128)(2,1)} %bitcast.25), kind=kOutput, calls=%fused_computation.17 | convolution fusion | flops 419430400 | bytes 3768320 | tf_op jit(solution)/shard_map/dot_general | solution.py:516
  127.1 0.3 slice_add_fusion
  127.4 0.1 slice_add_fusion.1
  127.5 0.2 copy.10
  127.7 0.2 copy.9
  127.8 0.1 subtract_bitcast_fusion
  128.0 0.9 pad_maximum_fusion
  (4 shorter events, 0.0 us)
Async XLA Ops:
  19.6 105.7 %copy-start = (bf16[1280,320]{1,0:T(8,128)(2,1)S(1)}, bf16[1280,320]{1,0:T(8,128)(2,1)}, u32[]{:S(2)}) copy-start(bf16[1280,320]{1,0:T(8,128)(2,1)} %constant.37.clone) | copy-start | bytes 2457604

commit v4 on v3

--- a/solution.py
+++ b/solution.py
@@ -20,7 +20,7 @@
     for axis, peers in groups:
         for peer in peers:
             pl.semaphore_signal(barrier, inc=1, device_id={axis: peer}, device_id_type=MESH)
-    pl.semaphore_wait(barrier, sum(len(peers) for _, peers in groups))
+    return sum(len(peers) for _, peers in groups)
 
 
 def remote(src, dst, send_sem, recv_sem, axis, peer):
@@ -95,6 +95,7 @@
     others = [lax.rem(chip + d, chips) for d in range(1, chips)]
     seats = [other * 2 + core for other in others]
     sources = [lax.rem(chip + chips - d, chips) for d in range(1, chips)]
+    greeted = greet(("pix", peers), ("elec", [partner] + seats))
     rows_a[...] = jnp.zeros_like(rows_a)
 
     def correlate(fields, start):
@@ -111,7 +112,7 @@
     lax.fori_loop(0, pixels // sub, opening, 0)
     for j in range(np_):
         part_ref[j] = rows_a[pl.ds(j * depth, depth), 0:electrons]
-    greet(("pix", peers), ("elec", [partner] + seats))
+    pl.semaphore_wait(pltpu.get_barrier_semaphore(), greeted)
     started = scatter_gather(
         np_, peers, part_ref, held_a, total_a, ps.at[0], ps.at[1], ps.at[2], ps.at[3]
     )
@@ -420,7 +421,7 @@
     chunk = order // ne
     depth = order // np_
     pieces = next(count for count in (4, 2, 1) if pixels % (128 * count) == 0)
-    sub = next(size for size in (512, 640, 256, 128) if pixels // pieces % size == 0)
+    sub = next(size for size in (1280, 640, 512, 256, 128) if pixels // pieces % size == 0)
     chips = ne // 2
     wide = electrons + order + -order % 128
     share = mode_count // ne

time: 129 us -> 122 us (0.946)
  Pallas kernels: 106 us -> 98.1 us
    pallas_call x1, Pallas kernels: 106 us -> 98.1 us  [middle(): pl.pallas_call(functools.partial(core_kernel, np_, ne, pieces, sub, elect...]
where the time goes in v4:
time: 122 us; the launch traced here: 121 us
  Pallas kernels  98.1 us (80%)
  local copies, waits for them, and re-layouts  16.9 us (14%)
  other arithmetic  4.43 us (4%)
  matrix products  1.81 us (1%)
    pallas_call x1, Pallas kernels, middle(): pl.pallas_call(functools.partial(core_kernel, np_, ne, pieces, sub, elect...  98.1 us
    unnamed x4, local copies, waits for them, and re-layouts  16.6 us

profile of v4, /device:TPU:0, one launch (start us, length us, event | category | flops | bytes accessed | tf_op | source)
XLA Modules:
  0.0 121.3 jit_solution(15609195082417405269)
XLA Ops:
  0.0 0.2 fusion.3
  0.3 0.6 pad_maximum_fusion.1.chirp_ref
  0.9 0.3 fusion.1
  1.2 1.9 %convert_element_type.18 = bf16[2,32,40,256]{3,2,1,0:T(8,128)(2,1)S(1)} convert(f32[2,32,40,256]{3,2,1,0:T(8,128)} %param.5) | non-fusion elementwise | flops 655360 | bytes 3932160 | tf_op jit(solution)/shard_map/convert_element_type | solution.py:537
  3.0 1.3 %copy.12 = bf16[8,8,40,256]{3,1,2,0:T(8,128)(2,1)} copy(bf16[8,8,40,256]{3,2,1,0:T(8,128)(2,1)S(1)} %bitcast.21) | data formatting | bytes 2621440
  4.4 15.2 %copy.11 = bf16[48,8,80,256]{3,1,2,0:T(8,128)(2,1)} copy(bf16[48,8,80,256]{3,2,1,0:T(8,128)(2,1)} %bitcast.20) | data formatting | bytes 31457280
  19.6 0.0 copy-start
  19.6 98.1 %middle.1 = bf16[8,40,512]{2,1,0:T(8,128)(2,1)} custom-call(bf16[384,20480]{1,0:T(8,128)(2,1)} %bitcast.19, bf16[64,10240]{1,0:T(8,128)(2,1)} %bitcast.22, f32[2,40,256]{2,1,0:T(8,128)} %pad_maximum_fusion.1.chirp_ref, bf16[2,512,512]{2,1,0:T(8,128)(2,1)} %constant.36.clone.table_ref), custom_call_target="tpu_custom_call" | custom-call | tf_op jit(solution)/shard_map/middle/pallas_call | solution.py:433
  117.7 0.0 copy-done
  117.7 1.8 %fusion.4 = f32[1280,512]{1,0:T(8,128)S(1)} fusion(bf16[1280,320]{1,0:T(8,128)(2,1)S(1)} %copy-done, bf16[320,512]{1,0:T(8,128)(2,1)} %bitcast.25), kind=kOutput, calls=%fused_computation.17 | convolution fusion | flops 419430400 | bytes 3768320 | tf_op jit(solution)/shard_map/dot_general | solution.py:517
  119.5 0.3 slice_add_fusion
  119.8 0.1 slice_add_fusion.1
  119.9 0.2 copy.10
  120.1 0.2 copy.9
  120.2 0.1 subtract_bitcast_fusion
  120.3 0.9 pad_maximum_fusion
  (4 shorter events, 0.0 us)
Async XLA Ops:
  19.6 98.1 %copy-start = (bf16[1280,320]{1,0:T(8,128)(2,1)S(1)}, bf16[1280,320]{1,0:T(8,128)(2,1)}, u32[]{:S(2)}) copy-start(bf16[1280,320]{1,0:T(8,128)(2,1)} %constant.37.clone) | copy-start | bytes 2457604
